TPU v7x, 32 devices: a whole 2x2x4 slice. The times are simulated.
32 devices in a mesh: dp: 8 (over z, x), tensor: 4 (over y, core).
Axes of the slice: x: 2, y: 2, z: 4, core: 2. Of those that a mesh axis runs over, the one named last changes fastest.
Arguments:
- block_input: bfloat16 [20480, 1536], P(('dp', 'tensor')), may hold values from -6 to 6
- seq_lengths: int32 [8, 5], P('dp'), may hold values from 1 to 1024, 2560 in all within a row
- w_qkv: float32 [768, 3, 768], P('dp', None, 'tensor'), may hold values from -0.21875 to 0.21875
- w_out: float32 [768, 768], P('dp', 'tensor'), may hold values from -0.875 to 0.875
- w_gate_up: float32 [768, 2, 3072], P('dp', None, 'tensor'), may hold values from -0.21875 to 0.21875
- w_down: float32 [768, 3072], P('dp', 'tensor'), may hold values from -0.109375 to 0.109375
- gain_attn: float32 [768], replicated, may hold values from 0.5 to 1.5
- gain_ffn: float32 [768], replicated, may hold values from 0.5 to 1.5
- mix_matrix: float32 [2, 2], replicated, may hold values from 0.3 to 1
- correct_gain: float32 [2], replicated, may hold values from 0.5 to 1.5
- cotangent: bfloat16 [20480, 1536], P(('dp', 'tensor')), may hold values from -6 to 6
Outputs:
- block_output: bfloat16 [20480, 1536], P(('dp', 'tensor'))
- grad_input: float32 [20480, 1536], P(('dp', 'tensor'))
- grad_w_qkv: float32 [768, 3, 768], P('dp', None, 'tensor')
- grad_w_out: float32 [768, 768], P('dp', 'tensor')
- grad_w_gate_up: float32 [768, 2, 3072], P('dp', None, 'tensor')
- grad_w_down: float32 [768, 3072], P('dp', 'tensor')
- grad_gain_attn: float32 [768], replicated
- grad_gain_ffn: float32 [768], replicated
- grad_mix_matrix: float32 [2, 2], replicated
- grad_correct_gain: float32 [2], replicated
Inputs may be any that keep to these rules, and one draw needn't show every extreme that they name: Each row of seq_lengths sums to 2560, and its largest entry is 1024.
All inputs are finite; a program needn't handle non-finite values.
Results may differ from a plain program's by a relative error of at most 0.014.
Values may be sent and summed in bfloat16 or wider, within the bound.
A program may use at most 192 MiB of HBM per device.

v0:
```python
import math

import jax
import jax.numpy as jnp
from jax import lax
from jax.sharding import PartitionSpec as P

HEAD_DIM = 64


EPS = 1e-06
BIG = 1e30


def split_up(array, dim, count):
    dims = array.shape
    blocks = array.reshape(*dims[:dim], count, dims[dim] // count, *dims[dim + 1 :])
    return jnp.moveaxis(blocks, dim, 0)


def sent_and_summed(array, axis, dim):
    blocks = split_up(array, dim, lax.axis_size(axis))
    arrived = lax.all_to_all(blocks, axis, split_axis=0, concat_axis=0, tiled=True)
    return arrived.astype(jnp.float32).sum(axis=0)


def sent_together(arrays, axis, dim, along):
    widths = [math.prod(a.shape[along:]) for a in arrays]
    both = jnp.concatenate(
        [a.reshape(*a.shape[:along], w) for a, w in zip(arrays, widths)], axis=along
    )
    result = sent_and_summed(both, axis, dim)
    blocks = jnp.split(result, [sum(widths[:k]) for k in range(1, len(widths))], axis=along)
    return tuple(
        (b.reshape(*result.shape[:along], *a.shape[along:]) for a, b in zip(arrays, blocks))
    )


def segment_of(lengths_row, total_rows):
    boundary = jnp.cumsum(lengths_row)
    position = jnp.arange(total_rows, dtype=jnp.int32)
    return jnp.sum((position[:, None] >= boundary[None, :]).astype(jnp.int32), axis=1)


def rms_norm(features, norm_gain):
    return (
        features
        * lax.rsqrt(jnp.mean(features * features, axis=-1, keepdims=True) + EPS)
        * norm_gain
    )


def norm_pull(features, norm_gain, incoming):
    _, norm_back = jax.vjp(rms_norm, features, norm_gain)
    return norm_back(incoming)


def block_mask(segment, position, first_row, block_rows, key_first, key_span):
    seg_rows = lax.dynamic_slice_in_dim(segment, first_row, block_rows, 0)
    pos_rows = lax.dynamic_slice_in_dim(position, first_row, block_rows, 0)
    seg_keys = lax.dynamic_slice_in_dim(segment, key_first, key_span, 0)
    pos_keys = lax.dynamic_slice_in_dim(position, key_first, key_span, 0)
    return (seg_rows[:, None] == seg_keys[None, :]) & (pos_keys[None, :] <= pos_rows[:, None])


def block_scores(query_rows, key_rows, allowed):
    scores = (
        jnp.einsum("qhe,khe->hqk", query_rows, key_rows, preferred_element_type=jnp.float32) * 0.125
    )
    return jnp.where(allowed[None], scores, -BIG)


def spread_rows(normed):
    return lax.all_gather(normed, "tensor", axis=0, tiled=True)


def again_rows(normed):
    return lax.all_gather(normed, "tensor", axis=0, tiled=True)


def spread_grads(incoming):
    return lax.all_gather(incoming.astype(jnp.bfloat16), "tensor", axis=0, tiled=True)


def back_rows(term_fn, local_rows):
    return lax.psum_scatter(
        term_fn(jnp.int32(0), local_rows * lax.axis_size("tensor")),
        "tensor",
        scatter_dimension=0,
        tiled=True,
    )


def local(
    block_input,
    seq_lengths,
    w_qkv,
    w_out,
    w_gate_up,
    w_down,
    gain_attn,
    gain_ffn,
    mix_matrix,
    correct_gain,
    cotangent,
):
    model_width = gain_attn.shape[0]
    local_rows = block_input.shape[0]
    group_rows = local_rows * lax.axis_size("tensor")
    heads_dev = w_qkv.shape[2] // HEAD_DIM
    head_features = heads_dev * HEAD_DIM
    inputs = block_input.astype(jnp.float32)
    stream_one = inputs[:, :model_width]
    stream_two = inputs[:, model_width:]
    predicted_main = mix_matrix[0, 0] * stream_one + mix_matrix[0, 1] * stream_two
    predicted_side = mix_matrix[1, 0] * stream_one + mix_matrix[1, 1] * stream_two
    attn_all, out_all = (
        lax.all_gather(w_qkv.astype(jnp.bfloat16), "dp", axis=0, tiled=True),
        lax.all_gather(w_out.astype(jnp.bfloat16), "dp", axis=0, tiled=True),
    )
    normed_attn = rms_norm(predicted_main, gain_attn).astype(jnp.bfloat16)
    normed_attn_all = spread_rows(normed_attn)
    projected = jnp.einsum(
        "td,dkh->tkh", normed_attn_all, attn_all, preferred_element_type=jnp.float32
    ).astype(jnp.bfloat16)
    queries = projected[:, 0].reshape(group_rows, heads_dev, HEAD_DIM)
    all_keys = projected[:, 1].reshape(group_rows, heads_dev, HEAD_DIM)
    values = projected[:, 2].reshape(group_rows, heads_dev, HEAD_DIM)
    block_rows = min(512, group_rows)
    block_count = group_rows // block_rows
    longest = min(1024, group_rows // 2)
    key_span = min(group_rows, block_rows + longest)
    lengths_row = seq_lengths[0]
    segment = segment_of(lengths_row, group_rows)
    seq_starts = jnp.cumsum(lengths_row) - lengths_row
    seq_numbers = jnp.arange(lengths_row.shape[0], dtype=jnp.int32)
    position = jnp.arange(group_rows, dtype=jnp.int32)
    first_rows = jnp.arange(block_count, dtype=jnp.int32) * block_rows

    def key_start(first_row):
        first_seg = lax.dynamic_slice_in_dim(segment, first_row, 1, 0)[0]
        begin = jnp.sum(jnp.where(seq_numbers == first_seg, seq_starts, 0))
        return jnp.minimum(begin, group_rows - key_span)

    def forward_block(first_row):
        key_first = key_start(first_row)
        query_rows = lax.dynamic_slice_in_dim(queries, first_row, block_rows, 0)
        key_rows = lax.dynamic_slice_in_dim(all_keys, key_first, key_span, 0)
        value_rows = lax.dynamic_slice_in_dim(values, key_first, key_span, 0)
        allowed = block_mask(segment, position, first_row, block_rows, key_first, key_span)
        scores = block_scores(query_rows, key_rows, allowed)
        row_max = jnp.max(scores, axis=-1, keepdims=True)
        weights_raw = jnp.exp(scores - row_max)
        row_total = jnp.sum(weights_raw, axis=-1, keepdims=True)
        attn_probs = (weights_raw / row_total).astype(jnp.bfloat16)
        attended = jnp.einsum(
            "hqk,khe->qhe", attn_probs, value_rows, preferred_element_type=jnp.float32
        )
        return (attended, row_max, row_total)

    attended, row_maxes, row_totals = lax.map(forward_block, first_rows)
    attn_heads = attended.reshape(group_rows, head_features).astype(jnp.bfloat16)
    row_piece = attn_heads
    attn_branch = lax.psum_scatter(
        lax.dot_general(
            row_piece, out_all, (((1,), (1,)), ((), ())), preferred_element_type=jnp.float32
        ),
        "tensor",
        scatter_dimension=0,
        tiled=True,
    )
    middle = predicted_main + attn_branch
    gate_all, down_all = (
        lax.all_gather(w_gate_up.astype(jnp.bfloat16), "dp", axis=0, tiled=True),
        lax.all_gather(w_down.astype(jnp.bfloat16), "dp", axis=0, tiled=True),
    )
    normed_ffn = rms_norm(middle, gain_ffn).astype(jnp.bfloat16)
    normed_ffn_all = spread_rows(normed_ffn)
    gate_up = jnp.einsum(
        "td,dkf->tkf", normed_ffn_all, gate_all, preferred_element_type=jnp.float32
    )
    gate_pre = gate_up[:, 0]
    up_proj = gate_up[:, 1]
    activated = jax.nn.gelu(gate_pre)
    hidden = (activated * up_proj).astype(jnp.bfloat16)
    row_piece = hidden
    ffn_branch = lax.psum_scatter(
        lax.dot_general(
            row_piece, down_all, (((1,), (1,)), ((), ())), preferred_element_type=jnp.float32
        ).astype(jnp.bfloat16),
        "tensor",
        scatter_dimension=0,
        tiled=True,
    ).astype(jnp.float32)
    layer_top = middle + ffn_branch
    correction = layer_top - predicted_main
    block_output = jnp.concatenate(
        [
            predicted_main + correct_gain[0] * correction,
            predicted_side + correct_gain[1] * correction,
        ],
        axis=1,
    ).astype(jnp.bfloat16)
    incoming = cotangent.astype(jnp.float32)
    cot_one = incoming[:, :model_width]
    cot_two = incoming[:, model_width:]
    grad_correct = jnp.stack([jnp.sum(cot_one * correction), jnp.sum(cot_two * correction)])
    grad_top = correct_gain[0] * cot_one + correct_gain[1] * cot_two
    gate_all, down_all = (
        lax.all_gather(w_gate_up.astype(jnp.bfloat16), "dp", axis=0, tiled=True),
        lax.all_gather(w_down.astype(jnp.bfloat16), "dp", axis=0, tiled=True),
    )
    normed_ffn_all = again_rows(normed_ffn)
    grad_ffn_all = spread_grads(grad_top)
    grad_hidden = jnp.dot(grad_ffn_all, down_all, preferred_element_type=jnp.float32)
    grad_down = lax.dot_general(
        grad_ffn_all, hidden, (((0,), (0,)), ((), ())), preferred_element_type=jnp.float32
    )
    _, gelu_pull = jax.vjp(jax.nn.gelu, gate_pre)
    grad_gate = gelu_pull(grad_hidden * up_proj)[0]
    grad_up = grad_hidden * activated
    grad_gate_up = jnp.stack([grad_gate, grad_up], axis=1).astype(jnp.bfloat16)
    weight_gate_up = jnp.einsum(
        "td,tkf->dkf", normed_ffn_all, grad_gate_up, preferred_element_type=jnp.float32
    )

    def ffn_back(first_row, row_count):
        return jnp.einsum("tkf,dkf->td", grad_gate_up, gate_all, preferred_element_type=jnp.float32)

    grad_normed_ffn = back_rows(ffn_back, local_rows)
    grad_middle_norm, grad_gain_ffn = norm_pull(middle, gain_ffn, grad_normed_ffn)
    grad_middle = grad_top + grad_middle_norm
    sum_gate_up, sum_down = (
        lax.psum_scatter(weight_gate_up, "dp", scatter_dimension=0, tiled=True),
        lax.psum_scatter(grad_down, "dp", scatter_dimension=0, tiled=True),
    )
    attn_all, out_all = (
        lax.all_gather(w_qkv.astype(jnp.bfloat16), "dp", axis=0, tiled=True),
        lax.all_gather(w_out.astype(jnp.bfloat16), "dp", axis=0, tiled=True),
    )
    normed_attn_all = again_rows(normed_attn)
    grad_attn_all = spread_grads(grad_middle)
    grad_heads = jnp.dot(grad_attn_all, out_all, preferred_element_type=jnp.float32).astype(
        jnp.bfloat16
    )
    grad_heads = grad_heads.reshape(group_rows, heads_dev, HEAD_DIM)
    grad_out = lax.dot_general(
        grad_attn_all, attn_heads, (((0,), (0,)), ((), ())), preferred_element_type=jnp.float32
    )

    def backward_block(running, block_item):
        first_row, row_max, row_total = block_item
        key_first = key_start(first_row)
        query_rows = lax.dynamic_slice_in_dim(queries, first_row, block_rows, 0)
        grad_rows = lax.dynamic_slice_in_dim(grad_heads, first_row, block_rows, 0)
        key_rows = lax.dynamic_slice_in_dim(all_keys, key_first, key_span, 0)
        value_rows = lax.dynamic_slice_in_dim(values, key_first, key_span, 0)
        allowed = block_mask(segment, position, first_row, block_rows, key_first, key_span)
        scores = block_scores(query_rows, key_rows, allowed)
        attn_probs = jnp.exp(scores - row_max) / row_total
        grad_probs = jnp.einsum(
            "qhe,khe->hqk", grad_rows, value_rows, preferred_element_type=jnp.float32
        )
        row_dot = jnp.sum(attn_probs * grad_probs, axis=-1, keepdims=True)
        grad_scores = (attn_probs * (grad_probs - row_dot)).astype(jnp.bfloat16)
        grad_query = (
            jnp.einsum("hqk,khe->qhe", grad_scores, key_rows, preferred_element_type=jnp.float32)
            * 0.125
        )
        grad_key = (
            jnp.einsum("hqk,qhe->khe", grad_scores, query_rows, preferred_element_type=jnp.float32)
            * 0.125
        )
        grad_value = jnp.einsum(
            "hqk,qhe->khe",
            attn_probs.astype(jnp.bfloat16),
            grad_rows,
            preferred_element_type=jnp.float32,
        )
        key_total = lax.dynamic_slice_in_dim(running[0], key_first, key_span, 0) + grad_key
        value_total = lax.dynamic_slice_in_dim(running[1], key_first, key_span, 0) + grad_value
        new_keys = lax.dynamic_update_slice_in_dim(running[0], key_total, key_first, 0)
        new_values = lax.dynamic_update_slice_in_dim(running[1], value_total, key_first, 0)
        return ((new_keys, new_values), grad_query)

    zero_keys = jnp.zeros((group_rows, heads_dev, HEAD_DIM), jnp.float32)
    (grad_keys, grad_values), grad_queries = lax.scan(
        backward_block, (zero_keys, zero_keys), (first_rows, row_maxes, row_totals)
    )
    grad_projected = jnp.stack(
        [
            grad_queries.reshape(group_rows, head_features),
            grad_keys.reshape(group_rows, head_features),
            grad_values.reshape(group_rows, head_features),
        ],
        axis=1,
    ).astype(jnp.bfloat16)
    weight_qkv = jnp.einsum(
        "td,tkh->dkh", normed_attn_all, grad_projected, preferred_element_type=jnp.float32
    )

    def attn_back(first_row, row_count):
        return jnp.einsum(
            "tkh,dkh->td", grad_projected, attn_all, preferred_element_type=jnp.float32
        )

    grad_normed_attn = back_rows(attn_back, local_rows)
    grad_main_norm, grad_gain_attn = norm_pull(predicted_main, gain_attn, grad_normed_attn)
    grad_main = cot_one + grad_middle + grad_main_norm - grad_top
    grad_input = jnp.concatenate(
        [
            mix_matrix[0, 0] * grad_main + mix_matrix[1, 0] * cot_two,
            mix_matrix[0, 1] * grad_main + mix_matrix[1, 1] * cot_two,
        ],
        axis=1,
    )
    grad_mix = jnp.stack(
        [
            jnp.stack([jnp.sum(grad_main * stream_one), jnp.sum(grad_main * stream_two)]),
            jnp.stack([jnp.sum(cot_two * stream_one), jnp.sum(cot_two * stream_two)]),
        ]
    )
    sum_qkv, sum_out = sent_together(
        (weight_qkv.astype(jnp.bfloat16), grad_out.astype(jnp.bfloat16)), "dp", 0, 1
    )
    total_gain_attn, total_gain_ffn, total_mix, total_correct = lax.psum(
        (grad_gain_attn, grad_gain_ffn, grad_mix, grad_correct), ("dp", "tensor")
    )
    return (
        block_output,
        grad_input,
        sum_qkv,
        sum_out,
        sum_gate_up,
        sum_down,
        total_gain_attn,
        total_gain_ffn,
        total_mix,
        total_correct,
    )


def solution(mesh):
    placed = (
        P(("dp", "tensor"), None),
        P("dp", None),
        P("dp", None, "tensor"),
        P("dp", "tensor"),
        P("dp", None, "tensor"),
        P("dp", "tensor"),
        P(),
        P(),
        P(),
        P(),
        P(("dp", "tensor"), None),
    )
    return jax.shard_map(
        local,
        mesh=mesh,
        in_specs=placed,
        out_specs=(
            P(("dp", "tensor"), None),
            P(("dp", "tensor"), None),
            P("dp", None, "tensor"),
            P("dp", "tensor"),
            P("dp", None, "tensor"),
            P("dp", "tensor"),
            P(),
            P(),
            P(),
            P(),
        ),
        check_vma=False,
    )
```

profile of v0, /device:TPU:0, one launch (start us, length us, event | category | flops | bytes accessed | tf_op | source)
XLA Modules:
  0.0 990.2 jit_solution(4468324045412369846)
XLA Ops:
  17.1 38.6 %all_gather.31 = bf16[768,3,192]{2,1,0:T(4,128)(2,1)S(1)} all-gather(bf16[96,3,192]{2,1,0:T(4,128)(2,1)S(1)} %copy.69), channel_id=1, replica_groups=mesh['dp'=8,'tensor'=4] {'dp'}, dimensions={0}, use_global_device_ids=true | all-gather | bytes 995328 | tf_op jit(solution)/shard_map/all_gather | solution.py:118
  57.8 31.3 %all_gather.32 = bf16[768,192]{1,0:T(8,128)(2,1)S(1)} all-gather(bf16[96,192]{1,0:T(8,128)(2,1)} %convert_element_type.86), channel_id=1, replica_groups=mesh['dp'=8,'tensor'=4] {'dp'}, dimensions={0}, use_global_device_ids=true | all-gather | bytes 331776 | tf_op jit(solution)/shard_map/all_gather | solution.py:119
  96.1 88.1 %while.32 = (s32[]{:T(128)}, bf16[5,512,3,64]{1,3,2,0:T(8,128)(2,1)S(1)}, f32[5,3,512,1]{2,1,3,0:T(4,128)}, f32[5,3,512,1]{2,1,3,0:T(4,128)}, s32[5]{0:T(128)S(1...) while((s32[]{:T(128)}, ...), condition=%wide.region_7.8_spmd.clone.clone, body=%wide.region_3.7_spmd.clone.clone.sunk | while | flops 634647552 | bytes 33339708 | solution.py:161
  192.4 66.9 %reduce-scatter.7.cloned.1.call-done = f32[640,768]{1,0:T(8,128)} async-done(((f32[2560,768]{1,0:T(8,128)}), f32[640,768]{1,0:T(8,128)}) %reduce-scatter.7.cloned.1.call-update) | async-done | bytes 1966096 | tf_op jit(solution)/shard_map/reduce_scatter | solution.py:164
  269.6 27.0 %all-gather.9.cloned.1.call-done = bf16[2560,768]{1,0:T(8,128)(2,1)} async-done(((bf16[640,768]{1,0:T(8,128)(2,1)}), bf16[2560,768]{1,0:T(8,128)(2,1)}) %all-gather.9.cloned.1.call-update) | async-done | bytes 3932176 | tf_op jit(solution)/shard_map/all_gather | solution.py:74
  296.6 11.9 %fusion.54 = f32[2560,2,768]{2,0,1:T(8,128)} fusion(bf16[768,2,768]{2,0,1:T(8,128)(2,1)} %all-gather.11.cloned.1.call-done, bf16[2560,768]{1,0:T(8,128)(2,1)} %all-gather.9.cloned.1.call-done), kind=kOutput, calls=%fused_computation.76 | convolution fusion | flops 6039797760 | bytes 22020096 | tf_op jit(solution)/shard_map/td,dkf->tkf/dot_general | solution.py:179
  308.5 32.2 %all-gather.13.cloned.1.call-done = bf16[768,768]{1,0:T(8,128)(2,1)} async-done(((bf16[96,768]{1,0:T(8,128)(2,1)}), bf16[768,768]{1,0:T(8,128)(2,1)}) %all-gather.13.cloned.1.call-update) | async-done | bytes 1179664 | tf_op jit(solution)/shard_map/all_gather | solution.py:175
  340.7 32.8 %all-gather.15.cloned.1.call-done = bf16[2560,768]{1,0:T(8,128)(2,1)} async-done(((bf16[640,768]{1,0:T(8,128)(2,1)}), bf16[2560,768]{1,0:T(8,128)(2,1)}) %all-gather.15.cloned.1.call-update) | async-done | bytes 3932176 | tf_op jit(solution)/shard_map/all_gather | solution.py:82
  373.5 15.0 %fusion.56 = (bf16[2560,1,768]{2,0,1:T(8,128)(2,1)S(1)}, bf16[2560,1,768]{2,0,1:T(8,128)(2,1)S(1)}, bf16[2560,768]{1,0:T(8,128)(2,1)}) fusion(f32[2560,2,768]{2,0,1:T(8,128)} %fusion.54, bf16[2560,768]{1,0:T(8,128)(2,1)} %all-gather.15.cloned.1.call-done, bf16[768,768]{1,0:T(8,128)(2,1)} %all-gather.13.cloned.1.call-done), kind=kOutput, calls=%fused_computation.78 | convolution fusion | flops 3071016960 | bytes 32636928 | tf_op jit(solution)/shard_map/dot_general | solution.py:215
  391.6 10.1 %convolution_bitcast_fusion = f32[2560,768]{1,0:T(8,128)} fusion(bf16[768,2,768]{2,0,1:T(8,128)(2,1)} %all-gather.11.cloned.1.call-done, bf16[2560,1,768]{2,0,1:T(8,128)(2,1)S(1)} %get-tuple-element.426, bf16[2560,1,768]{2,0,1:T(8,128)(2,1)S(1)} %get-tuple-element.425), kind=kOutput, calls=%fused_computation.69 | convolution fusion | flops 6043729920 | bytes 18087936 | tf_op jit(solution)/shard_map/tkf,dkf->td/dot_general | solution.py:228
  401.8 69.5 %reduce-scatter.11.cloned.1.call-done = f32[640,768]{1,0:T(8,128)} async-done(((f32[2560,768]{1,0:T(8,128)}), f32[640,768]{1,0:T(8,128)}) %reduce-scatter.11.cloned.1.call-update) | async-done | bytes 1966096 | tf_op jit(solution)/shard_map/reduce_scatter | solution.py:86
  475.6 11.3 %fusion.51 = f32[768,2,768]{2,0,1:T(8,128)} fusion(bf16[2560,1,768]{2,0,1:T(8,128)(2,1)} %copy-done.43, bf16[2560,1,768]{2,0,1:T(8,128)(2,1)} %copy-done.42, bf16[2560,768]{1,0:T(8,128)(2,1)} %all-gather.9.cloned.1.call-done), kind=kOutput, calls=%fused_computation.72 | convolution fusion | flops 6055526400 | bytes 16515072 | tf_op jit(solution)/shard_map/td,tkf->dkf/dot_general | solution.py:223
  487.0 21.7 %all-gather.17.cloned.1.call-done = bf16[2560,768]{1,0:T(8,128)(2,1)} async-done(((bf16[640,768]{1,0:T(8,128)(2,1)}), bf16[2560,768]{1,0:T(8,128)(2,1)}) %all-gather.17.cloned.1.call-update) | async-done | bytes 3932176 | tf_op jit(solution)/shard_map/all_gather | solution.py:82
  516.0 255.0 %while.33 = (s32[]{:T(128)}, f32[2560,3,64]{0,2,1:T(8,128)}, f32[2560,3,64]{0,2,1:T(8,128)S(1)}, bf16[5,512,3,64]{1,3,2,0:T(8,128)(2,1)}, s32[5]{0:T(128)S(1)}, ...) while((s32[]{:T(128)}, f32[2560,3,64]{0,2,1:T(8,128)}, ...), condition=%wide.region_16.17_spmd.clone.clone, body=%wide.region_13.16_spmd.clone.clone.sunk | while | flops 1536883200 | bytes 141459904 | solution.py:287
  525.7 8.7 multiply_reduce_fusion.14
  534.4 9.6 multiply_convert_fusion.6
  544.0 4.9 fusion.129
  548.9 5.6 dynamic_update_slice.45
  554.5 4.9 fusion.130
  562.2 7.7 dynamic_update_slice.44
  579.5 8.7 multiply_reduce_fusion.14
  588.2 9.5 multiply_convert_fusion.6
  602.4 5.6 dynamic_update_slice.45
  608.0 4.9 fusion.130
  615.4 7.7 dynamic_update_slice.44
  632.6 8.6 multiply_reduce_fusion.14
  641.3 9.5 multiply_convert_fusion.6
  658.1 4.9 fusion.130
  665.4 7.0 dynamic_update_slice.44
  682.0 8.6 multiply_reduce_fusion.14
  690.6 9.5 multiply_convert_fusion.6
  707.5 4.9 fusion.130
  714.8 7.0 dynamic_update_slice.44
  731.3 8.6 multiply_reduce_fusion.14
  739.9 9.5 multiply_convert_fusion.6
  756.7 4.9 fusion.130
  764.0 7.0 dynamic_update_slice.44
  780.1 5.4 convolution_bitcast_fusion.1
  786.7 7.4 convolution_convert_fusion
  809.2 14.7 %all-to-all-start = ((bf16[8,96,768]{2,1,0:T(8,128)(2,1)}), bf16[8,96,768]{2,1,0:T(8,128)(2,1)S(1)}, u32[]{:S(2)}, u32[]{:S(2)}) async-start(bf16[8,96,768]{2,1,0:T(8,128)(2,1)} %copy.75), calls=%async_computation.4 | async-start | bytes 2359296 | tf_op jit(solution)/shard_map/all_to_all | solution.py:23
  824.2 8.0 fusion.72
  834.7 18.2 %all-to-all-done = bf16[8,96,768]{2,1,0:T(8,128)(2,1)S(1)} async-done(((bf16[8,96,768]{2,1,0:T(8,128)(2,1)}), bf16[8,96,768]{2,1,0:T(8,128)(2,1)S(1)}, u32[]{:S(2)}, u32[]{:S(2)}) %all-to-all-start) | async-done | bytes 1179680 | tf_op jit(solution)/shard_map/all_to_all | solution.py:23
  854.9 8.2 reduce-scatter.13.cloned.1.call-done
  865.2 43.1 %reduce-scatter.9.cloned.1.call-done = bf16[640,768]{1,0:T(8,128)(2,1)} async-done(((bf16[2560,768]{1,0:T(8,128)(2,1)}), bf16[640,768]{1,0:T(8,128)(2,1)}) %reduce-scatter.9.cloned.1.call-update) | async-done | bytes 983056 | tf_op jit(solution)/shard_map/reduce_scatter | solution.py:187
  908.3 9.4 multiply_reduce_fusion.2
  921.7 40.0 %all-reduce = (f32[768]{0:T(1024)}, f32[768]{0:T(1024)}, f32[2,2]{1,0:T(2,128)}, f32[2]{0:T(128)}) all-reduce(f32[768]{0:T(1024)S(1)} %get-tuple-element.353, f32[768]{0:T(1024)S(1)} %copy-done.37, f32[2,2]{1,0:T(2,128)S(1)} %pad_maximum_fusion.7, f32[2]{0:T(128)S(1)} %pad_maximum_fusion.8), channel_id=1, replica_groups=mesh['dp'=8,'tensor'=4] {'dp','tensor'}, use_global_device_ids=true, to_apply=%region_23.24 | all-reduce | flops 1542 | bytes 12336 | tf_op jit(solution)/shard_map/psum | solution.py:326
  961.8 6.1 add_convert_fusion.1
  976.2 6.2 reduce-scatter.17.cloned.1.call-done
  (318 shorter events, 244.6 us)
Async XLA Ops:
  8.0 81.1 %all-gather.7.cloned.1.call-start = ((), (), s32[]{:S(2)}) async-start(), calls=%async_computation.7 | async-start | bytes 4915200 | tf_op jit(solution)/shard_map/all_gather | solution.py:74
  11.6 3.2 copy-start.33
  13.6 245.8 %copy-start.2 = (f32[640,768]{1,0:T(8,128)}, f32[640,768]{1,0:T(8,128)S(1)}, u32[]{:S(2)}) copy-start(f32[640,768]{1,0:T(8,128)S(1)} %get-tuple-element.416) | copy-start | bytes 5898244
  13.6 2.7 copy-start.26
  13.6 3.3 copy-start.22
  16.0 243.3 %reduce-scatter.7.cloned.1.call-start = ((), (), s32[]{:S(2)}) async-start(), calls=%async_computation.8 | async-start | bytes 9830400 | tf_op jit(solution)/shard_map/reduce_scatter | solution.py:164
  190.6 79.0 %all-gather.11.cloned.1.call-start = ((), (), s32[]{:S(2)}) async-start(), calls=%async_computation.10 | async-start | bytes 2654208 | tf_op jit(solution)/shard_map/all_gather | solution.py:174
  192.4 70.1 %copy-start.27 = (f32[768]{0:T(1024)S(1)}, f32[768]{0:T(1024)}, u32[]{:S(2)}) copy-start(f32[768]{0:T(1024)} %param.22) | copy-start | bytes 9220
  192.4 104.2 %all-gather.9.cloned.1.call-start = ((), (), s32[]{:S(2)}) async-start(), calls=%async_computation.9 | async-start | bytes 4915200 | tf_op jit(solution)/shard_map/all_gather | solution.py:74
  261.2 3.6 copy-start.19
  261.2 212.8 %copy-start.24 = (f32[640]{0:T(1024)}, f32[640]{0:T(1024)S(1)}, u32[]{:S(2)}) copy-start(f32[640]{0:T(1024)S(1)} %fusion.62) | copy-start | bytes 7684
  263.7 77.0 %all-gather.13.cloned.1.call-start = ((), (), s32[]{:S(2)}) async-start(), calls=%async_computation.11 | async-start | bytes 1327104 | tf_op jit(solution)/shard_map/all_gather | solution.py:175
  264.4 109.1 %all-gather.15.cloned.1.call-start = ((), (), s32[]{:S(2)}) async-start(), calls=%async_computation.13 | async-start | bytes 4915200 | tf_op jit(solution)/shard_map/all_gather | solution.py:82
  265.4 4.1 copy-start.7
  269.5 201.7 %reduce-scatter.11.cloned.1.call-start = ((), (), s32[]{:S(2)}) async-start(), calls=%async_computation.14 | async-start | bytes 9830400 | tf_op jit(solution)/shard_map/reduce_scatter | solution.py:86
  388.5 3.1 copy-start.43
  401.7 69.5 %copy-start.6 = (f32[640,768]{1,0:T(8,128)S(1)}, f32[640,768]{1,0:T(8,128)}, u32[]{:S(2)}) copy-start(f32[640,768]{1,0:T(8,128)} %copy-done.5) | copy-start | bytes 5898244
  401.7 107.0 %all-gather.17.cloned.1.call-start = ((), (), s32[]{:S(2)}) async-start(), calls=%async_computation.15 | async-start | bytes 4915200 | tf_op jit(solution)/shard_map/all_gather | solution.py:82
  471.2 2.8 copy-start.9
  471.2 2.8 copy-start.10
  475.6 356.7 %reduce-scatter.15.cloned.1.call-start = ((), (), s32[]{:S(2)}) async-start(), calls=%async_computation.17 | async-start | bytes 5308416 | tf_op jit(solution)/shard_map/reduce_scatter | solution.py:234
  487.0 376.1 %reduce-scatter.13.cloned.1.call-start = ((), (), s32[]{:S(2)}) async-start(), calls=%async_computation.16 | async-start | bytes 9830400 | tf_op jit(solution)/shard_map/reduce_scatter | solution.py:86
  525.7 8.7 copy-start
  554.5 4.9 copy-start.1
  579.5 8.7 copy-start
  608.0 4.9 copy-start.1
  632.6 8.6 copy-start
  658.1 4.9 copy-start.1
  682.0 8.6 copy-start
  707.4 4.9 copy-start.1
  731.2 8.6 copy-start
  756.7 4.9 copy-start.1
  776.8 3.3 copy-start.20
  785.5 122.8 %reduce-scatter.9.cloned.1.call-start = ((), (), s32[]{:S(2)}) async-start(), calls=%async_computation.12 | async-start | bytes 4915200 | tf_op jit(solution)/shard_map/reduce_scatter | solution.py:187
  795.3 5.4 copy-start.15
  795.3 5.4 copy-start.17
  809.2 43.7 %all-to-all-start = ((bf16[8,96,768]{2,1,0:T(8,128)(2,1)}), bf16[8,96,768]{2,1,0:T(8,128)(2,1)S(1)}, u32[]{:S(2)}, u32[]{:S(2)}) async-start(bf16[8,96,768]{2,1,0:T(8,128)(2,1)} %copy.75), calls=%async_computation.4 | async-start | bytes 2359296 | tf_op jit(solution)/shard_map/all_to_all | solution.py:23
  823.9 158.5 %reduce-scatter.17.cloned.1.call-start = ((), (), s32[]{:S(2)}) async-start(), calls=%async_computation.18 | async-start | bytes 2654208 | tf_op jit(solution)/shard_map/reduce_scatter | solution.py:235
  832.2 30.9 %copy-start.3 = (f32[640,768]{1,0:T(8,128)S(1)}, f32[640,768]{1,0:T(8,128)}, u32[]{:S(2)}) copy-start(f32[640,768]{1,0:T(8,128)} %copy-done.2) | copy-start | bytes 5898244
  832.2 30.9 %copy-start.30 = (f32[640]{0:T(1024)S(1)}, f32[640]{0:T(1024)}, u32[]{:S(2)}) copy-start(f32[640]{0:T(1024)} %copy-done.29) | copy-start | bytes 7684
  832.2 30.9 %copy-start.34 = (f32[768]{0:T(1024)S(1)}, f32[768]{0:T(1024)}, u32[]{:S(2)}) copy-start(f32[768]{0:T(1024)} %param.21) | copy-start | bytes 9220
  853.1 12.1 %copy-start.36 = (f32[640]{0:T(1024)S(1)}, f32[640]{0:T(1024)}, u32[]{:S(2)}) copy-start(f32[640]{0:T(1024)} %copy-done.35) | copy-start | bytes 7684
  853.1 55.3 %copy-start.25 = (f32[640]{0:T(1024)S(1)}, f32[640]{0:T(1024)}, u32[]{:S(2)}) copy-start(f32[640]{0:T(1024)} %copy-done.24) | copy-start | bytes 7684
  853.1 55.3 %copy-start.28 = (f32[768]{0:T(1024)S(1)}, f32[768]{0:T(1024)}, u32[]{:S(2)}) copy-start(f32[768]{0:T(1024)} %param.22) | copy-start | bytes 9220
  853.1 55.2 %copy-start.32 = (f32[640]{0:T(1024)S(1)}, f32[640]{0:T(1024)}, u32[]{:S(2)}) copy-start(f32[640]{0:T(1024)} %copy-done.31) | copy-start | bytes 7684
  865.2 56.5 %copy-start.37 = (f32[768]{0:T(1024)S(1)}, f32[768]{0:T(1024)}, u32[]{:S(2)}) copy-start(f32[768]{0:T(1024)} %get-tuple-element.351) | copy-start | bytes 9220
  961.8 7.6 copy-start.11
  967.9 2.8 copy-start.8
  (17 other events, 25.2 us)
Sparse Core Ops, SparseCore 0:
  16.1 35.6 all-gather.6
  190.7 68.6 reduce-scatter.6
  475.7 32.9 all-gather.16
Sparse Core Ops, SparseCore 1:
  193.8 50.8 all-gather.10
  263.8 32.8 all-gather.8
  299.2 41.4 all-gather.12
  342.3 31.2 all-gather.14
  401.8 69.4 reduce-scatter.10
  487.1 95.7 reduce-scatter.14
  785.6 77.5 reduce-scatter.12
  865.5 42.7 reduce-scatter.8
  912.3 70.1 reduce-scatter.16
where the time goes:
time: 1000 us; the launch traced here: 990 us
  waiting for transfers between devices  326 us (33%)
  matrix products  247 us (25%)
  other arithmetic  132 us (13%)
  local copies, waits for them, and re-layouts  116 us (12%)
  blocking collectives  110 us (11%)
  loops' own time  26.6 us (3%)
  between operations  16.5 us (2%)
  starting transfers between devices  16 us (2%)
    reduce_scatter x2, waiting for transfers between devices, back_rows(): lax.psum_scatter(term_fn(jnp.int32(0), local_rows * lax.axis_size('tensor...  77.7 us
    reduce_scatter x1, waiting for transfers between devices, local(): lax.psum_scatter(lax.dot_general(row_piece, out_all, (((1,), (1,)), ((),...  66.9 us
    dot_general x10, matrix products, block_scores(): jnp.einsum('qhe,khe->hqk', query_rows, key_rows, preferred_element_type=j...  61.3 us
    all_gather x2, waiting for transfers between devices, spread_grads(): lax.all_gather(incoming.astype(jnp.bfloat16), 'tensor', axis=0, tiled=True)  54.5 us
    convert_element_type x5, other arithmetic, backward_block(): grad_scores = (attn_probs * (grad_probs - row_dot)).astype(jnp.bfloat16)  47.4 us
    reduce_scatter x1, waiting for transfers between devices, local(): lax.psum_scatter(lax.dot_general(row_piece, down_all, (((1,), (1,)), ((),...  43.1 us
    psum x1, blocking collectives, local(): lax.psum((grad_gain_attn, grad_gain_ffn, grad_mix, grad_correct), ('dp',...  40 us
    all_gather x1, blocking collectives, local(): lax.all_gather(w_qkv.astype(jnp.bfloat16), 'dp', axis=0, tiled=True)  38.6 us
  transfers between devices with their start and end apart: 13, of which 10 were waited for; matrix products, arithmetic and copies ran while one was open for 36% of the time, Pallas kernels for 0%

commit v1 on v0

v1 whole, which is shorter than its diff:
```python
import functools
import math

import jax
import jax.numpy as jnp
from jax import lax
from jax.experimental import pallas as pl
from jax.experimental.pallas import tpu as pltpu
from jax.sharding import PartitionSpec as P

HEAD_DIM = 64
EPS = 1e-06
BIG = 1e30
BLK = 256
SUB = 128
MESH = pl.DeviceIdType.MESH


def dot(a, b):
    return jnp.dot(a, b, preferred_element_type=jnp.float32)


def dot_nt(a, b):
    return lax.dot_general(a, b, (((1,), (1,)), ((), ())), preferred_element_type=jnp.float32)


def dot_tn(a, b):
    return lax.dot_general(a, b, (((0,), (0,)), ((), ())), preferred_element_type=jnp.float32)


def turned(a):
    return a.astype(jnp.float32).T


def seg_vector(len_ref, pos):
    begin = jnp.zeros_like(pos)
    edge = jnp.int32(0)
    for k in range(len_ref.shape[1] - 1):
        edge = edge + len_ref[0, k]
        begin = jnp.where(pos >= edge, edge, begin)
    return begin


def seg_scalar(len_ref, row):
    begin = jnp.int32(0)
    end = jnp.int32(0)
    edge = jnp.int32(0)
    for k in range(len_ref.shape[1]):
        after = edge + len_ref[0, k]
        inside = (row >= edge) & (row < after)
        begin = jnp.where(inside, edge, begin)
        end = jnp.where(inside, after, end)
        edge = after
    return begin, end


def place(me, chunk, per):
    return (chunk // per) ^ me, pl.multiple_of((chunk % per) * SUB, SUB)


def fwd_kernel(heads, parts, len_ref, me_ref, *refs):
    proj = refs[:parts]
    o_ref, ot_ref, lse_ref, qt, kh, vt, acc, mx, tot = refs[parts:]
    i = pl.program_id(0)
    part_rows = proj[0].shape[0]
    per = part_rows // SUB
    blk, hd = BLK, HEAD_DIM
    feats = heads * hd
    me = me_ref[0]

    @pl.when(i == 0)
    def _():
        for c in range(parts):
            base = (me ^ c) * part_rows
            def turn(s, carry, c=c, base=base):
                src = pl.ds(pl.multiple_of(s * SUB, SUB), SUB)
                at = pl.ds(pl.multiple_of(base + s * SUB, SUB), SUB)
                rows = proj[c][src, :]
                qt[:, at] = (turned(rows[:, :feats]) * 0.125).astype(jnp.bfloat16)
                vt[:, at] = turned(rows[:, 2 * feats :]).astype(jnp.bfloat16)
                for h in range(heads):
                    kh[h, at, :] = rows[:, feats + h * hd : feats + (h + 1) * hd]
                return carry
            lax.fori_loop(0, per, turn, 0)

    first = pl.multiple_of(i * blk, blk)
    cols = pl.ds(first, blk)
    pos = first + lax.broadcasted_iota(jnp.int32, (1, blk), 1)
    begin = seg_vector(len_ref, pos)
    b_first, _ = seg_scalar(len_ref, first)
    b_last, _ = seg_scalar(len_ref, first + blk - 1)
    j_lo = b_first // blk
    j_full = jnp.minimum((b_last + blk - 1) // blk, i)
    mx[...] = jnp.full_like(mx, -BIG)
    tot[...] = jnp.zeros_like(tot)
    acc[...] = jnp.zeros_like(acc)

    def step(j, masked, first_pass):
        at = pl.ds(pl.multiple_of(j * blk, blk), blk)
        if masked:
            key = j * blk + lax.broadcasted_iota(jnp.int32, (blk, blk), 0)
            ok = (key >= begin) & (key <= pos)
        scores = []
        for h in range(heads):
            s = dot(kh[h, at, :], qt[h * hd : (h + 1) * hd, cols])
            scores.append(jnp.where(ok, s, -BIG) if masked else s)
        if first_pass:
            for h in range(heads):
                old = mx[h : h + 1]
                new = jnp.maximum(old, jnp.max(scores[h], axis=0, keepdims=True))
                total = jnp.sum(jnp.exp(scores[h] - new), axis=0, keepdims=True)
                mx[h : h + 1] = new
                tot[h : h + 1] = jnp.exp(old - new) * tot[h : h + 1] + total
        else:
            for h in range(heads):
                hs = slice(h * hd, (h + 1) * hd)
                p = jnp.exp(scores[h] - mx[h : h + 1])
                acc[hs] += dot(vt[hs, at], p.astype(jnp.bfloat16))

    def loop(lo, hi, masked, first_pass):
        def body(j, carry):
            step(j, masked, first_pass)
            return carry
        lax.fori_loop(lo, hi, body, 0)

    for first_pass in (True, False):
        loop(j_lo, j_full, True, first_pass)
        loop(jnp.maximum(j_full, j_lo), i, False, first_pass)
        step(i, True, first_pass)
        if first_pass:
            mx[...] = mx[...] + jnp.log(tot[...])
            lse_ref[...] = mx[...]
    ot_ref[...] = acc[...]
    out = acc[...].T.astype(jnp.bfloat16)
    for s in range(blk // SUB):
        c, row = place(me, i * (blk // SUB) + s, per)
        o_ref[c, pl.ds(row, SUB), :] = out[s * SUB : (s + 1) * SUB]


def attn_fwd(lengths, me, proj):
    parts = len(proj)
    part_rows, width = proj[0].shape
    feats = width // 3
    rows = parts * part_rows
    heads = feats // HEAD_DIM
    return pl.pallas_call(
        functools.partial(fwd_kernel, heads, parts),
        out_shape=(
            jax.ShapeDtypeStruct((parts, part_rows, feats), jnp.bfloat16),
            jax.ShapeDtypeStruct((feats, rows), jnp.float32),
            jax.ShapeDtypeStruct((8, rows), jnp.float32),
        ),
        grid_spec=pltpu.PrefetchScalarGridSpec(
            num_scalar_prefetch=2,
            grid=(rows // BLK,),
            in_specs=[pl.BlockSpec((part_rows, width), lambda i, s, m: (0, 0))] * parts,
            out_specs=(
                pl.BlockSpec((parts, part_rows, feats), lambda i, s, m: (0, 0, 0)),
                pl.BlockSpec((feats, BLK), lambda i, s, m: (0, i)),
                pl.BlockSpec((8, BLK), lambda i, s, m: (0, i)),
            ),
            scratch_shapes=[
                pltpu.VMEM((feats, rows), jnp.bfloat16),
                pltpu.VMEM((heads, rows, HEAD_DIM), jnp.bfloat16),
                pltpu.VMEM((feats, rows), jnp.bfloat16),
                pltpu.VMEM((feats, BLK), jnp.float32),
                pltpu.VMEM((8, BLK), jnp.float32),
                pltpu.VMEM((8, BLK), jnp.float32),
            ],
        ),
        cost_estimate=pl.CostEstimate(
            flops=rows * feats * 4096, bytes_accessed=12 * rows * feats, transcendentals=rows * 512 * heads
        ),
        name="attn_fwd",
    )(lengths, me, *proj)


def bwd_kernel(heads, parts, len_ref, me_ref, *refs):
    proj = refs[:parts]
    grads = refs[parts : 2 * parts]
    ot_ref, lse_ref, d_ref, qt, qp, gt, gp, kh, vh, kt, dqt, delta, dkv = refs[2 * parts :]
    j = pl.program_id(0)
    n = pl.num_programs(0)
    part_rows = proj[0].shape[0]
    per = part_rows // SUB
    blk, hd = BLK, HEAD_DIM
    feats = heads * hd
    me = me_ref[0]

    @pl.when(j == 0)
    def _():
        zero = jnp.zeros((SUB, hd), jnp.bfloat16)
        for c in range(parts):
            base = (me ^ c) * part_rows
            def turn(s, carry, c=c, base=base):
                src = pl.ds(pl.multiple_of(s * SUB, SUB), SUB)
                at = pl.ds(pl.multiple_of(base + s * SUB, SUB), SUB)
                rows = proj[c][src, :]
                g = grads[c][src, :]
                g_turned = turned(g)
                qt[:, at] = (turned(rows[:, :feats]) * 0.125).astype(jnp.bfloat16)
                kt[:, at] = turned(rows[:, feats : 2 * feats]).astype(jnp.bfloat16)
                gt[:, at] = g_turned.astype(jnp.bfloat16)
                prod = g_turned * ot_ref[:, at]
                dqt[:, at] = jnp.zeros((feats, SUB), jnp.float32)
                for h in range(heads):
                    hs = slice(h * hd, (h + 1) * hd)
                    delta[h : h + 1, at] = jnp.sum(prod[hs], axis=0, keepdims=True)
                    qp[h, at, :] = jnp.concatenate([rows[:, hs], zero], axis=1)
                    gp[h, at, :] = jnp.concatenate([zero, g[:, hs]], axis=1)
                    kh[h, at, :] = rows[:, feats + h * hd : feats + (h + 1) * hd]
                    vh[h, at, :] = rows[:, 2 * feats + h * hd : 2 * feats + (h + 1) * hd]
                return carry
            lax.fori_loop(0, per, turn, 0)

    first = pl.multiple_of(j * blk, blk)
    keys = pl.ds(first, blk)
    _, e_first = seg_scalar(len_ref, first)
    _, e_last = seg_scalar(len_ref, first + blk - 1)
    i_hi = (e_last - 1) // blk + 1
    i_full = jnp.clip(e_first // blk, j + 1, i_hi)
    key = first + lax.broadcasted_iota(jnp.int32, (blk, blk), 0)

    def step(i, masked, start):
        at = pl.ds(pl.multiple_of(i * blk, blk), blk)
        if masked:
            pos = i * blk + lax.broadcasted_iota(jnp.int32, (1, blk), 1)
            begin = seg_vector(len_ref, pos)
            ok = (key >= begin) & (key <= pos)
        scores, dprobs = [], []
        for h in range(heads):
            hs = slice(h * hd, (h + 1) * hd)
            scores.append(dot(kh[h, keys, :], qt[hs, at]))
            dprobs.append(dot(vh[h, keys, :], gt[hs, at]))
        both = []
        for h in range(heads):
            e = scores[h] - lse_ref[h : h + 1, at]
            if masked:
                e = jnp.where(ok, e, -BIG)
            p = jnp.exp(e)
            ds = p * (dprobs[h] - delta[h : h + 1, at])
            both.append((p.astype(jnp.bfloat16), ds.astype(jnp.bfloat16)))
        for h in range(heads):
            hs = slice(h * hd, (h + 1) * hd)
            p, ds = both[h]
            add = dot(
                jnp.concatenate([ds, p], axis=1),
                jnp.concatenate([qp[h, at, :], gp[h, at, :]], axis=0),
            )
            if start:
                dkv[h] = add
            else:
                dkv[h] += add
            dqt[hs, at] += dot(kt[hs, keys], ds)

    def loop(lo, hi, masked):
        def body(i, carry):
            step(i, masked, False)
            return carry
        lax.fori_loop(lo, hi, body, 0)

    step(j, True, True)
    loop(j + 1, i_full, False)
    loop(i_full, i_hi, True)
    pair = jnp.concatenate(
        [dkv[h][:, :hd] * 0.125 for h in range(heads)] + [dkv[h][:, hd:] for h in range(heads)], axis=1
    ).astype(jnp.bfloat16)
    for s in range(blk // SUB):
        c, row = place(me, j * (blk // SUB) + s, per)
        d_ref[c, pl.ds(row, SUB), feats:] = pair[s * SUB : (s + 1) * SUB]

    @pl.when(j == n - 1)
    def _():
        for c in range(parts):
            base = (me ^ c) * part_rows
            def turn(s, carry, c=c, base=base):
                at = pl.ds(pl.multiple_of(base + s * SUB, SUB), SUB)
                dst = pl.ds(pl.multiple_of(s * SUB, SUB), SUB)
                d_ref[c, dst, :feats] = (dqt[:, at] * 0.125).T.astype(jnp.bfloat16)
                return carry
            lax.fori_loop(0, per, turn, 0)


def attn_bwd(lengths, me, proj, grads, heads_turned, log_total):
    parts = len(proj)
    part_rows, width = proj[0].shape
    feats = width // 3
    rows = parts * part_rows
    heads = feats // HEAD_DIM
    return pl.pallas_call(
        functools.partial(bwd_kernel, heads, parts),
        out_shape=jax.ShapeDtypeStruct((parts, part_rows, width), jnp.bfloat16),
        grid_spec=pltpu.PrefetchScalarGridSpec(
            num_scalar_prefetch=2,
            grid=(rows // BLK,),
            in_specs=[pl.BlockSpec((part_rows, width), lambda i, s, m: (0, 0))] * parts
            + [pl.BlockSpec((part_rows, feats), lambda i, s, m: (0, 0))] * parts
            + [
                pl.BlockSpec((feats, rows), lambda i, s, m: (0, 0)),
                pl.BlockSpec((8, rows), lambda i, s, m: (0, 0)),
            ],
            out_specs=pl.BlockSpec((parts, part_rows, width), lambda i, s, m: (0, 0, 0)),
            scratch_shapes=[
                pltpu.VMEM((feats, rows), jnp.bfloat16),
                pltpu.VMEM((heads, rows, 2 * HEAD_DIM), jnp.bfloat16),
                pltpu.VMEM((feats, rows), jnp.bfloat16),
                pltpu.VMEM((heads, rows, 2 * HEAD_DIM), jnp.bfloat16),
                pltpu.VMEM((heads, rows, HEAD_DIM), jnp.bfloat16),
                pltpu.VMEM((heads, rows, HEAD_DIM), jnp.bfloat16),
                pltpu.VMEM((feats, rows), jnp.bfloat16),
                pltpu.VMEM((feats, rows), jnp.float32),
                pltpu.VMEM((8, rows), jnp.float32),
                pltpu.VMEM((heads, BLK, 2 * HEAD_DIM), jnp.float32),
            ],
        ),
        cost_estimate=pl.CostEstimate(
            flops=rows * feats * 10240, bytes_accessed=20 * rows * feats, transcendentals=rows * 512 * heads
        ),
        name="attn_bwd",
    )(lengths, me, *proj, *grads, heads_turned, log_total)


def gelu_parts(v):
    c = math.sqrt(2 / math.pi)
    square = v * v
    t = jnp.tanh(c * v * (1.0 + 0.044715 * square))
    half = 0.5 * (1.0 + t)
    slope = half + (0.5 * v) * (1.0 - t * t) * (c * (1.0 + 3 * 0.044715 * square))
    return v * half, slope


def ffn_kernel(tile, x_ref, g_ref, wg_ref, wu_ref, wd_ref, h_ref, dg_ref, du_ref, branch_ref, dx_ref, branch, dx):
    u = pl.program_id(0)
    x = x_ref[...]
    gate = dot(x, wg_ref[...])
    up = dot(x, wu_ref[...])
    grad_hidden = dot(g_ref[...], wd_ref[...])
    act, slope = gelu_parts(gate)
    hidden = (act * up).astype(jnp.bfloat16)
    dgate = (slope * (grad_hidden * up)).astype(jnp.bfloat16)
    dup = (grad_hidden * act).astype(jnp.bfloat16)
    h_ref[...] = hidden
    dg_ref[...] = dgate
    du_ref[...] = dup
    b_add = dot_nt(hidden, wd_ref[...])
    d_add = dot_nt(dgate, wg_ref[...]) + dot_nt(dup, wu_ref[...])

    @pl.when(u == 0)
    def _():
        branch[...] = b_add
        dx[...] = d_add

    @pl.when(u > 0)
    def _():
        branch[...] += b_add
        dx[...] += d_add

    @pl.when(u == pl.num_programs(0) - 1)
    def _():
        branch_ref[...] = branch[...]
        dx_ref[...] = dx[...].astype(jnp.bfloat16)


def ffn_rows(x, g, weights, tile=256):
    rows, d = x.shape
    units = weights.shape[1] // 3
    n = units // tile
    full = pl.BlockSpec((rows, d), lambda u: (0, 0))
    cols = pl.BlockSpec((rows, tile), lambda u: (0, u))
    wide = jax.ShapeDtypeStruct((rows, units), jnp.bfloat16)
    narrow = jax.ShapeDtypeStruct((rows, d), jnp.bfloat16)
    return pl.pallas_call(
        functools.partial(ffn_kernel, tile),
        out_shape=(wide, wide, wide, jax.ShapeDtypeStruct((rows, d), jnp.float32), narrow),
        grid=(n,),
        in_specs=[
            full,
            full,
            pl.BlockSpec((d, tile), lambda u: (0, u)),
            pl.BlockSpec((d, tile), lambda u: (0, u + n)),
            pl.BlockSpec((d, tile), lambda u: (0, u + 2 * n)),
        ],
        out_specs=(cols, cols, cols, full, full),
        scratch_shapes=[pltpu.VMEM((rows, d), jnp.float32), pltpu.VMEM((rows, d), jnp.float32)],
        cost_estimate=pl.CostEstimate(
            flops=12 * rows * d * units,
            bytes_accessed=2 * (4 * rows * d + 3 * rows * units + 3 * d * units),
            transcendentals=rows * units,
        ),
        name="ffn_rows",
    )(x, g, weights, weights, weights)


def wgrad_kernel(parts, n, *refs):
    xs, gs, gates, ups, hiddens = [refs[parts * m : parts * (m + 1)] for m in range(5)]
    out, left_t = refs[-2:]
    i = pl.program_id(0)
    rows = xs[0].shape[0]

    def turn_all(lefts):
        for c in range(parts):
            def turn(s, carry, c=c):
                src = pl.ds(pl.multiple_of(s * SUB, SUB), SUB)
                at = pl.ds(pl.multiple_of(c * rows + s * SUB, SUB), SUB)
                left_t[:, at] = turned(lefts[c][src, :]).astype(jnp.bfloat16)
                return carry
            lax.fori_loop(0, rows // SUB, turn, 0)

    def product(rights):
        total = dot(left_t[:, :rows], rights[0][...])
        for c in range(1, parts):
            total += dot(left_t[:, c * rows : (c + 1) * rows], rights[c][...])
        out[...] = total.astype(jnp.bfloat16)

    @pl.when(i == 0)
    def _():
        turn_all(xs)

    @pl.when(i == 2 * n)
    def _():
        turn_all(gs)

    @pl.when(i < n)
    def _():
        product(gates)

    @pl.when((i >= n) & (i < 2 * n))
    def _():
        product(ups)

    @pl.when(i >= 2 * n)
    def _():
        product(hiddens)


def wgrad(xs, gs, gates, ups, hiddens, tile=256):
    parts = len(xs)
    rows, d = xs[0].shape
    units = gates[0].shape[1]
    n = units // tile

    def tiles(m):
        return [pl.BlockSpec((rows, tile), lambda i: (0, jnp.clip(i - m * n, 0, n - 1)))] * parts

    return pl.pallas_call(
        functools.partial(wgrad_kernel, parts, n),
        out_shape=jax.ShapeDtypeStruct((d, 3 * units), jnp.bfloat16),
        grid=(3 * n,),
        in_specs=[pl.BlockSpec((rows, d), lambda i: (0, 0))] * (2 * parts) + tiles(0) + tiles(1) + tiles(2),
        out_specs=pl.BlockSpec((d, tile), lambda i: (0, i)),
        scratch_shapes=[pltpu.VMEM((d, parts * rows), jnp.bfloat16)],
        cost_estimate=pl.CostEstimate(
            flops=6 * parts * rows * d * units,
            bytes_accessed=2 * parts * rows * (2 * d + 3 * units) + 6 * d * units,
            transcendentals=0,
        ),
        name="wgrad",
    )(*xs, *gs, *gates, *ups, *hiddens)


def rms_norm(features, norm_gain):
    return features * lax.rsqrt(jnp.mean(features * features, axis=-1, keepdims=True) + EPS) * norm_gain


def norm_pull(features, norm_gain, incoming):
    rate = lax.rsqrt(jnp.mean(features * features, axis=-1, keepdims=True) + EPS)
    scaled = norm_gain * incoming
    dot_mean = jnp.mean(scaled * features, axis=-1, keepdims=True)
    grad = rate * scaled - features * (rate * rate * rate * dot_mean)
    return grad, jnp.sum(incoming * features * rate, axis=0)


def swap(array, bit):
    count = lax.axis_size("tensor")
    return lax.ppermute(array, "tensor", [(i, i ^ bit) for i in range(count)])


def after(value, *others):
    return lax.optimization_barrier((value, *others))[0]


def flipped(index, bits):
    bit = 1
    while bit <= bits:
        if bits & bit:
            index = index + bit - 2 * bit * lax.rem(lax.div(index, bit), 2)
        bit *= 2
    return index


def start_kernel(
    count, chunks, x, qkv, wo, sib, far, diag, qkv_all, wo_all,
    local_sem, sib_sem, far_send, far_recv, diag_send, diag_recv, wo_send, wo_recv, qkv_dp, wo_dp,
):
    t = lax.axis_index("tensor")
    g = lax.axis_index("dp")
    order = []
    bit = 2
    while bit < count:
        order.append(bit)
        bit *= 2
    order.append(1)

    def last(e):
        return max(k for k, b in enumerate(order) if e & b)

    barrier = pltpu.get_barrier_semaphore()
    for c in (1, 2, 3):
        pl.semaphore_signal(barrier, inc=1, device_id={"tensor": flipped(t, c)}, device_id_type=MESH)
    for b in order:
        pl.semaphore_signal(barrier, inc=1, device_id={"dp": flipped(g, b)}, device_id_type=MESH)
    pl.semaphore_wait(barrier, 3 + len(order))

    size = x.shape[0] // chunks

    def far_copy(k):
        rows = pl.ds(k * size, size)
        return pltpu.make_async_remote_copy(
            x.at[rows], far.at[rows], far_send.at[k], far_recv.at[k], {"tensor": flipped(t, 2)}, MESH
        )

    def diag_copy(k):
        rows = pl.ds(k * size, size)
        return pltpu.make_async_remote_copy(
            far.at[rows], diag.at[rows], diag_send.at[k], diag_recv.at[k], {"tensor": flipped(t, 1)}, MESH
        )

    def wo_copy(c):
        return pltpu.make_async_remote_copy(
            wo, wo_all.at[c, g], wo_send.at[c - 1], wo_recv.at[c - 1], {"tensor": flipped(t, c)}, MESH
        )

    def dp_copy(which, e):
        b = order[last(e)]
        block = flipped(g, e ^ b)
        if which == 0:
            src = qkv if e == b else qkv_all.at[block]
            dst, sems = qkv_all.at[block], qkv_dp
        else:
            src = dst = wo_all.at[:, block]
            sems = wo_dp
        return pltpu.make_async_remote_copy(
            src, dst, sems.at[0, e - 1], sems.at[1, e - 1], {"dp": flipped(g, b)}, MESH
        )

    def dp_arrival(which, e):
        block = flipped(g, e)
        dst, sems = (qkv_all.at[block], qkv_dp) if which == 0 else (wo_all.at[:, block], wo_dp)
        return pltpu.make_async_remote_copy(
            dst, dst, sems.at[0, e - 1], sems.at[1, e - 1], {"dp": flipped(g, order[last(e)])}, MESH
        )

    sends = []

    def go(copy):
        copy.start()
        sends.append(copy)

    wos = [wo_copy(c) for c in (1, 2, 3)]
    for copy in wos:
        go(copy)
    for b in order:
        go(dp_copy(0, b))
    fars = [far_copy(k) for k in range(chunks)]
    for copy in fars:
        go(copy)
    near = pltpu.make_async_remote_copy(
        x, sib, sib_sem.at[0], sib_sem.at[1], {"tensor": flipped(t, 1)}, MESH
    )
    go(near)
    kept = [
        pltpu.make_async_copy(qkv, qkv_all.at[g], local_sem.at[0]),
        pltpu.make_async_copy(wo, wo_all.at[0, g], local_sem.at[1]),
    ]
    for copy in kept:
        copy.start()
    for copy in kept:
        copy.wait()
    for copy in wos:
        copy.wait_recv()
    for b in order:
        go(dp_copy(1, b))
    diags = []

    def pass_on(k):
        fars[k].wait_recv()
        diags.append(diag_copy(k))
        go(diags[-1])

    done = 0
    for e in sorted(range(1, count), key=lambda e: (last(e), e)):
        for which in (0, 1):
            dp_arrival(which, e).wait_recv()
            for b in order[last(e) + 1 :]:
                go(dp_copy(which, e ^ b))
        if done < chunks and e & 1 == 0:
            pass_on(done)
            done += 1
    while done < chunks:
        pass_on(done)
        done += 1
    for copy in diags:
        copy.wait_recv()
    near.wait_recv()
    for copy in sends:
        copy.wait_send()


def start(x, qkv, wo, chunks=4):
    count = lax.axis_size("dp")
    rows = jax.ShapeDtypeStruct(x.shape, x.dtype)
    dma = pltpu.SemaphoreType.DMA
    sib, far, diag, qkv_all, wo_all = pl.pallas_call(
        functools.partial(start_kernel, count, chunks),
        out_shape=(
            rows,
            rows,
            rows,
            jax.ShapeDtypeStruct((count, *qkv.shape), qkv.dtype),
            jax.ShapeDtypeStruct((4, count, *wo.shape), wo.dtype),
        ),
        in_specs=[pl.BlockSpec(memory_space=pl.ANY)] * 3,
        out_specs=(pl.BlockSpec(memory_space=pl.ANY),) * 5,
        scratch_shapes=[
            dma((2,)),
            dma((2,)),
            dma((chunks,)),
            dma((chunks,)),
            dma((chunks,)),
            dma((chunks,)),
            dma((3,)),
            dma((3,)),
            dma((2, count - 1)),
            dma((2, count - 1)),
        ],
        compiler_params=pltpu.CompilerParams(collective_id=0, has_side_effects=True),
        cost_estimate=pl.CostEstimate(flops=0, bytes_accessed=100_000_000, transcendentals=0),
        name="start",
    )(x, qkv, wo)
    whole = count * qkv.shape[0]
    return [x, sib, far, diag], qkv_all.reshape(whole, -1), [wo_all[c].reshape(whole, -1) for c in range(4)]


def spread(rows):
    far = swap(rows, 2)
    return [rows, swap(rows, 1), far, swap(far, 1)]


def exchange(blocks):
    return [blocks[0]] + [swap(blocks[c], c) for c in range(1, len(blocks))]


def summed(shares, before=None, beside=None):
    f32 = jnp.float32
    far = (shares[2].astype(f32) + swap(shares[3], 1).astype(f32)).astype(jnp.bfloat16)
    if before is not None:
        far = after(far, before)
    got = swap(far, 2)
    near = shares[0].astype(f32) + swap(shares[1], 1).astype(f32)
    if beside is not None:
        got, beside = lax.optimization_barrier((got, beside(far)))
    return near + got.astype(f32), beside


def sum_everywhere(array):
    for axis in ("tensor", "dp"):
        count = lax.axis_size(axis)
        bit = 1
        while bit < count:
            array = array + lax.ppermute(array, axis, [(i, i ^ bit) for i in range(count)])
            bit *= 2
    return array


def local(
    block_input, seq_lengths, w_qkv, w_out, w_gate_up, w_down, gain_attn, gain_ffn, mix_matrix, correct_gain, cotangent
):
    f32, bf16 = jnp.float32, jnp.bfloat16
    width = gain_attn.shape[0]
    me = lax.axis_index("tensor").astype(jnp.int32)[None]
    shard = w_qkv.shape[0]
    feats = w_out.shape[1]
    inputs = block_input.astype(f32)
    stream_one = inputs[:, :width]
    stream_two = inputs[:, width:]
    predicted_main = mix_matrix[0, 0] * stream_one + mix_matrix[0, 1] * stream_two
    predicted_side = mix_matrix[1, 0] * stream_one + mix_matrix[1, 1] * stream_two
    units = w_down.shape[1]

    normed_attn, qkv_all, out_parts = start(
        rms_norm(predicted_main, gain_attn).astype(bf16),
        w_qkv.reshape(shard, 3 * feats).astype(bf16),
        w_out.astype(bf16),
    )
    ffn_mine = jnp.concatenate([w_gate_up.reshape(shard, -1), w_down], axis=1).astype(bf16)
    ffn_all = lax.all_gather(after(ffn_mine, normed_attn[1]), "dp", axis=0, tiled=True)
    proj = [dot(x, qkv_all).astype(bf16) for x in normed_attn]
    attended, heads_turned, log_total = attn_fwd(seq_lengths, me, proj)

    incoming = cotangent.astype(f32)
    cot_one = incoming[:, :width]
    cot_two = incoming[:, width:]
    grad_top = correct_gain[0] * cot_one + correct_gain[1] * cot_two
    grad_ffn = spread(after(grad_top.astype(bf16), normed_attn[1]))

    attended = after(attended, grad_ffn[2])
    head_parts = exchange([attended[c] for c in range(len(proj))])
    attn_branch = sum(dot_nt(a, w) for a, w in zip(head_parts, out_parts))
    middle = predicted_main + attn_branch

    normed_mine = rms_norm(middle, gain_ffn).astype(bf16)
    normed_ffn = [normed_mine, swap(normed_mine, 1), swap(normed_mine, 2)]
    pieces = [ffn_rows(x, g, ffn_all) for x, g in zip(normed_ffn, grad_ffn[:2])]
    normed_ffn[2] = after(normed_ffn[2], pieces[0][0], pieces[1][0])
    normed_ffn.append(swap(normed_ffn[2], 1))
    pieces += [ffn_rows(x, g, ffn_all) for x, g in zip(normed_ffn[2:], grad_ffn[2:])]
    hidden, dgate, dup, branch, dnormed = zip(*pieces)
    grad_normed_ffn, weight_ffn = summed(
        dnormed, beside=lambda far: wgrad([after(normed_ffn[0], far)] + normed_ffn[1:], grad_ffn, dgate, dup, hidden)
    )
    weight_ffn = lax.psum_scatter(weight_ffn, "dp", scatter_dimension=0, tiled=True)
    grad_middle_norm, grad_gain_ffn = norm_pull(middle, gain_ffn, grad_normed_ffn)
    grad_middle = grad_top + grad_middle_norm
    grad_attn = grad_middle.astype(bf16)
    grad_heads = exchange([dot(grad_attn, w).astype(bf16) for w in out_parts])
    grad_proj = attn_bwd(seq_lengths, me, proj, grad_heads, heads_turned, log_total)
    *late, later_attn = lax.optimization_barrier((*head_parts, grad_heads[2], grad_heads[3], grad_attn))
    out_shares = exchange([dot_tn(later_attn, a).astype(bf16) for a in late[:4]])
    weight_out = sum(s.astype(f32) for s in out_shares)
    ffn_branch, (grad_proj, weight_out) = summed(branch, before=late[4], beside=lambda far: (grad_proj, weight_out))
    grad_proj = [grad_proj[c] for c in range(len(proj))]

    correction = (middle + ffn_branch) - predicted_main
    block_output = jnp.concatenate(
        [predicted_main + correct_gain[0] * correction, predicted_side + correct_gain[1] * correction], axis=1
    ).astype(bf16)
    grad_correct = jnp.stack([jnp.sum(cot_one * correction), jnp.sum(cot_two * correction)])

    far = [dot_nt(g, qkv_all).astype(bf16) for g in grad_proj[2:]]
    far = (far[0].astype(f32) + swap(far[1], 1).astype(f32)).astype(bf16)
    half = far.shape[0] // 2
    got = [swap(far[:half], 2), swap(far[half:], 2)]
    *late, far = lax.optimization_barrier((*grad_proj, *normed_attn, weight_out, far))
    near = [dot_nt(g, qkv_all).astype(bf16) for g in late[:2]]
    weight_qkv = sum(dot_tn(x, g) for x, g in zip(late[4:8], late[:4]))
    last = jnp.concatenate([weight_qkv, late[8]], axis=1).astype(bf16)
    last = last.reshape(lax.axis_size("dp"), shard, -1)
    last, weight_ffn, got[0] = lax.optimization_barrier((last, weight_ffn, got[0]))
    last = lax.all_to_all(last, "dp", split_axis=0, concat_axis=0, tiled=True)
    near = near[0].astype(f32) + swap(near[1], 1).astype(f32)
    got[1], last, near, grad_correct, block_output = lax.optimization_barrier(
        (got[1], last, near, grad_correct, block_output)
    )
    grad_normed_attn = near + jnp.concatenate(got, axis=0).astype(f32)
    weight_ffn = weight_ffn.astype(f32)
    sum_gate_up = weight_ffn[:, : 2 * units].reshape(shard, 2, units)
    sum_down = weight_ffn[:, 2 * units :]
    last = last.astype(f32).sum(axis=0)
    sum_qkv = last[:, : 3 * feats].reshape(shard, 3, feats)
    sum_out = last[:, 3 * feats :]

    grad_main_norm, grad_gain_attn = norm_pull(predicted_main, gain_attn, grad_normed_attn)
    grad_main = cot_one + grad_middle + grad_main_norm - grad_top
    grad_input = jnp.concatenate(
        [
            mix_matrix[0, 0] * grad_main + mix_matrix[1, 0] * cot_two,
            mix_matrix[0, 1] * grad_main + mix_matrix[1, 1] * cot_two,
        ],
        axis=1,
    )
    small = jnp.stack(
        [
            jnp.sum(grad_main * stream_one),
            jnp.sum(grad_main * stream_two),
            jnp.sum(cot_two * stream_one),
            jnp.sum(cot_two * stream_two),
            grad_correct[0],
            grad_correct[1],
        ]
    )
    small = jnp.stack([grad_gain_attn, grad_gain_ffn, jnp.pad(small, (0, width - small.shape[0]))])
    small = sum_everywhere(small)
    return (
        block_output,
        grad_input,
        sum_qkv,
        sum_out,
        sum_gate_up,
        sum_down,
        small[0],
        small[1],
        small[2, :4].reshape(2, 2),
        small[2, 4:6],
    )


def solution(mesh):
    placed = (
        P(("dp", "tensor"), None),
        P("dp", None),
        P("dp", None, "tensor"),
        P("dp", "tensor"),
        P("dp", None, "tensor"),
        P("dp", "tensor"),
        P(),
        P(),
        P(),
        P(),
        P(("dp", "tensor"), None),
    )
    return jax.shard_map(
        local,
        mesh=mesh,
        in_specs=placed,
        out_specs=(
            P(("dp", "tensor"), None),
            P(("dp", "tensor"), None),
            P("dp", None, "tensor"),
            P("dp", "tensor"),
            P("dp", None, "tensor"),
            P("dp", "tensor"),
            P(),
            P(),
            P(),
            P(),
        ),
        check_vma=False,
    )
```

time: 1000 us -> 395 us (0.40)
  waiting for transfers between devices: 326 us -> 44.8 us
  matrix products: 247 us -> 37.7 us
  Pallas kernels: 0 us -> 180 us
  blocking collectives: 110 us -> 0 us
  local copies, waits for them, and re-layouts: 116 us -> 35.2 us
  other arithmetic: 132 us -> 56.1 us
  loops' own time: 26.6 us -> 0 us
    dot_general x45 -> x24, matrix products: 240 us -> 37.7 us  [the longest x8 15.8 us: dot(): return jnp.dot(a, b, preferred_element_type=jnp.float32)]
    reduce_scatter x6 -> x1, waiting for transfers between devices: 194 us -> 0.01 us  [local(): lax.psum_scatter(weight_ffn, 'dp', scatter_dimension=0, tiled=True)]
    pallas_call x0 -> x8, Pallas kernels: none -> 180 us  [the longest x1 44.2 us: start(): pl.pallas_call(functools.partial(start_kernel, count, chunks), out_shape=...]
    all_gather x6 -> x1, waiting for transfers between devices: 114 us -> 0.01 us  [local(): lax.all_gather(after(ffn_mine, normed_attn[1]), 'dp', axis=0, tiled=True)]
    all_gather x2 -> x0, blocking collectives: 69.9 us -> none  [the longest x1 38.6 us: local(): lax.all_gather(w_qkv.astype(jnp.bfloat16), 'dp', axis=0, tiled=True)]
    dynamic_update_slice x15 -> x0, local copies, waits for them, and re-layouts: 58.4 us -> none  [the longest x5 36.4 us: backward_block(): lax.dynamic_update_slice_in_dim(running[0], key_total, key_first, 0)]
    convert_element_type x16 -> x10, other arithmetic: 58.9 us -> 17.9 us  [the longest x2 5.77 us: summed(): (shares[2].astype(f32) + swap(shares[3], 1).astype(f32)).astype(jnp.bfloa...]
    ppermute x0 -> x30, waiting for transfers between devices: none -> 41 us  [the longest x25 38.1 us: swap(): return lax.ppermute(array, 'tensor', [(i, i ^ bit) for i in range(count)])]
  transfers between devices with their start and end apart: 13 -> 33, of which waited for: 10 -> 13; matrix products, arithmetic and copies ran while one was open for 36% -> 24% of each run, Pallas kernels for 0% -> 32%
where the time goes in v1:
time: 395 us; the launch traced here: 392 us
  Pallas kernels  180 us (46%)
  other arithmetic  56.1 us (14%)
  waiting for transfers between devices  44.8 us (11%)
  matrix products  37.7 us (10%)
  local copies, waits for them, and re-layouts  35.2 us (9%)
  starting transfers between devices  23.2 us (6%)
  between operations  15 us (4%)
    pallas_call x1, Pallas kernels, start(): pl.pallas_call(functools.partial(start_kernel, count, chunks), out_shape=...  44.2 us
    pallas_call x4, Pallas kernels, ffn_rows(): pl.pallas_call(functools.partial(ffn_kernel, tile), out_shape=(wide, wide...  43 us
    ppermute x25, waiting for transfers between devices, swap(): return lax.ppermute(array, 'tensor', [(i, i ^ bit) for i in range(count)])  38.1 us
    pallas_call x1, Pallas kernels, attn_bwd(): pl.pallas_call(functools.partial(bwd_kernel, heads, parts), out_shape=jax...  34 us
    pallas_call x1, Pallas kernels, attn_fwd(): pl.pallas_call(functools.partial(fwd_kernel, heads, parts), out_shape=(ja...  33.5 us
    pallas_call x1, Pallas kernels, wgrad(): pl.pallas_call(functools.partial(wgrad_kernel, parts, n), out_shape=jax.S...  24.9 us
    dot_general x8, matrix products, dot(): return jnp.dot(a, b, preferred_element_type=jnp.float32)  15.8 us
    ppermute x25, starting transfers between devices, swap(): return lax.ppermute(array, 'tensor', [(i, i ^ bit) for i in range(count)])  14.7 us
  transfers between devices with their start and end apart: 33, of which 13 were waited for; matrix products, arithmetic and copies ran while one was open for 24% of the time, Pallas kernels for 32%

profile of v1, /device:TPU:0, one launch (start us, length us, event | category | flops | bytes accessed | tf_op | source)
XLA Modules:
  0.0 391.5 jit_solution(7415268314809611541)
XLA Ops:
  14.0 1.8 multiply_reduce_fusion.11
  17.9 44.2 %start.1 = (bf16[640,768]{1,0:T(8,128)(2,1)}, bf16[640,768]{1,0:T(8,128)(2,1)}, bf16[640,768]{1,0:T(8,128)(2,1)}, bf16[8,96,576]{2,1,0:T(8,128)(2,1)}, bf16[4,8,96,192]{3,2,1,0:T(8,128)(2,1)}) custom-call(bf16[640,768]{1,0:T(8,128)(2,1)} %multiply_convert_fusion.1.x, bf16[96,576]{1,0:T(8,128)(2,1)} %copy.59.qkv, bf16[96,192]{1,0:T(8,128)(2,1)} %convert_element_type.144.wo), custom_call_target="tpu_custom_call" | custom-call | bytes 100000000 | tf_op jit(solution)/shard_map/start/pallas_call | solution.py:613
  62.2 2.1 convert_element_type.149
  65.0 3.3 fusion.9
  70.2 3.4 convolution_convert_fusion.6.refs_1_
  73.6 1.8 convolution_convert_fusion.7.refs_0_
  75.4 1.8 convolution_convert_fusion.4.refs_3_
  77.3 1.9 convolution_convert_fusion.5.refs_2_
  79.1 33.5 %attn_fwd.1 = (bf16[4,640,192]{2,1,0:T(8,128)(2,1)}, f32[192,2560]{1,0:T(8,128)}, f32[8,2560]{1,0:T(8,128)}) custom-call(s32[1,5]{1,0:T(1,128)} %len_ref.3, s32[1]{0:T(128)} %bitcast.2.me_ref, bf16[640,576]{1,0:T(8,128)(2,1)} %convolution_convert_fusion.7.refs_0_, bf16[640,576]{1,0:T(8,128)(2,1)} %convolution_convert_fusion.6.refs_1_, ...), custom_call_target="tpu_custom_call" | custom-call | flops 2013265920 | bytes 5898240 | tf_op jit(solution)/shard_map/attn_fwd/pallas_call | solution.py:146
  119.0 13.4 %collective-permute-done.2 = bf16[640,192]{1,0:T(8,128)(2,1)S(1)} collective-permute-done((bf16[640,192]{1,0:T(8,128)(2,1)S(1)}, bf16[640,192]{1,0:T(8,128)(2,1)S(1)}, u32[]{:S(2)}, u32[]{:S(2)}) %collective-permute-start.2) | collective-permute-done | bytes 245792 | tf_op jit(solution)/shard_map/ppermute | solution.py:475
  136.6 10.6 %ffn_rows.4 = (bf16[640,768]{1,0:T(8,128)(2,1)}, bf16[640,768]{1,0:T(8,128)(2,1)}, bf16[640,768]{1,0:T(8,128)(2,1)}, f32[640,768]{1,0:T(8,128)}, bf16[640,768]{1,0:T(8,128)(2,1)}) custom-call(bf16[640,768]{1,0:T(8,128)(2,1)} %copy-done.43, bf16[640,768]{1,0:T(8,128)(2,1)} %get-tuple-element.75.g_ref.refs_4_, ...), custom_call_target="tpu_custom_call" | custom-call | flops 4529848320 | bytes 10420224 | tf_op jit(solution)/shard_map/ffn_rows/pallas_call | solution.py:372
  147.3 10.7 %ffn_rows.5 = (bf16[640,768]{1,0:T(8,128)(2,1)}, bf16[640,768]{1,0:T(8,128)(2,1)}, bf16[640,768]{1,0:T(8,128)(2,1)}, f32[640,768]{1,0:T(8,128)}, bf16[640,768]{1,0:T(8,128)(2,1)}) custom-call(bf16[640,768]{1,0:T(8,128)(2,1)} %collective-permute-done.5.x_ref.refs_1_, bf16[640,768]{1,0:T(8,128)(2,1)} %collective-permute-done.6.g_ref.refs_5_, ...), custom_call_target="tpu_custom_call" | custom-call | flops 4529848320 | bytes 10420224 | tf_op jit(solution)/shard_map/ffn_rows/pallas_call | solution.py:372
  158.0 2.0 collective-permute-done.4.x_ref.refs_2_
  160.0 2.8 collective-permute-done.7.x_ref.refs_3_
  163.8 11.0 %ffn_rows.7 = (bf16[640,768]{1,0:T(8,128)(2,1)}, bf16[640,768]{1,0:T(8,128)(2,1)}, bf16[640,768]{1,0:T(8,128)(2,1)}, f32[640,768]{1,0:T(8,128)}, bf16[640,768]{1,0:T(8,128)(2,1)}) custom-call(bf16[640,768]{1,0:T(8,128)(2,1)} %copy-done.49, bf16[640,768]{1,0:T(8,128)(2,1)} %collective-permute-done.8.g_ref.refs_7_, ...), custom_call_target="tpu_custom_call" | custom-call | flops 4529848320 | bytes 10420224 | tf_op jit(solution)/shard_map/ffn_rows/pallas_call | solution.py:372
  175.0 10.6 %ffn_rows.6 = (bf16[640,768]{1,0:T(8,128)(2,1)}, bf16[640,768]{1,0:T(8,128)(2,1)}, bf16[640,768]{1,0:T(8,128)(2,1)}, f32[640,768]{1,0:T(8,128)}, bf16[640,768]{1,0:T(8,128)(2,1)}) custom-call(bf16[640,768]{1,0:T(8,128)(2,1)} %collective-permute-done.4.x_ref.refs_2_, bf16[640,768]{1,0:T(8,128)(2,1)} %collective-permute-done.g_ref.refs_6_, ...), custom_call_target="tpu_custom_call" | custom-call | flops 4529848320 | bytes 10420224 | tf_op jit(solution)/shard_map/ffn_rows/pallas_call | solution.py:372
  185.6 2.4 add_convert_fusion.3
  189.1 24.9 %wgrad.1 = bf16[768,2304]{1,0:T(8,128)(2,1)} custom-call(bf16[640,768]{1,0:T(8,128)(2,1)} %copy-done.43, bf16[640,768]{1,0:T(8,128)(2,1)} %collective-permute-done.5.x_ref.refs_1_, bf16[640,768]{1,0:T(8,128)(2,1)} %collective-permute-done.4.x_ref.refs_2_, bf16[640,768]{1,0:T(8,128)(2,1)} %copy-done.49, bf16[640,768]{1,0:T(8,128)(2,1)} %get-tuple-element.75.g_ref.refs_4_, ...), custom_call_target="tpu_custom_call" | custom-call | flops 9059696640 | bytes 23199744 | tf_op jit(solution)/shard_map/wgrad/pallas_call | solution.py:445
  215.2 3.1 multiply_reduce_fusion.4
  218.9 2.2 fusion.8
  222.4 1.8 copy.67.refs_4_
  224.2 2.2 convolution_convert_fusion.14
  226.4 1.8 copy.64
  228.3 2.2 convolution_convert_fusion.13
  230.5 1.8 copy.65
  236.6 3.4 add_convert_fusion.4
  241.4 3.2 collective-permute-done.16.refs_7_
  244.6 7.3 %collective-permute-done.15.refs_6_ = bf16[640,192]{1,0:T(8,128)(2,1)S(1)} collective-permute-done((bf16[640,192]{1,0:T(8,128)(2,1)}, bf16[640,192]{1,0:T(8,128)(2,1)S(1)}, u32[]{:S(2)}, u32[]{:S(2)}) %collective-permute-start.15) | collective-permute-done | bytes 245792 | tf_op jit(solution)/shard_map/ppermute | solution.py:475
  258.0 34.0 %attn_bwd.1 = bf16[4,640,576]{2,1,0:T(8,128)(2,1)} custom-call(s32[1,5]{1,0:T(1,128)} %len_ref.3, s32[1]{0:T(128)} %bitcast.2.me_ref, bf16[640,576]{1,0:T(8,128)(2,1)} %convolution_convert_fusion.7.refs_0_, bf16[640,576]{1,0:T(8,128)(2,1)} %convolution_convert_fusion.6.refs_1_, bf16[640,576]{1,0:T(8,128)(2,1)} %convolution_convert_fusion.5.refs_2_, ...), custom_call_target="tpu_custom_call" | custom-call | flops 5033164800 | bytes 9830400 | tf_op jit(solution)/shard_map/attn_bwd/pallas_call | solution.py:290
  292.0 2.4 fusion.3
  294.5 2.3 convolution_convert_fusion.2
  297.3 1.8 slice_bitcast_fusion.2
  303.8 2.0 fusion.16
  308.8 2.0 add_convert_fusion.5
  312.3 2.3 pad_maximum_fusion.2
  315.8 4.5 %all-to-all-start = ((bf16[8,96,768]{2,1,0:T(8,128)(2,1)}), bf16[8,96,768]{2,1,0:T(8,128)(2,1)}, u32[]{:S(2)}, u32[]{:S(2)}) async-start(bf16[8,96,768]{2,1,0:T(8,128)(2,1)} %pad_maximum_fusion.2), calls=%async_computation.1 | async-start | bytes 2359296 | tf_op jit(solution)/shard_map/all_to_all | solution.py:749
  320.3 2.3 convolution_convert_fusion
  322.8 4.5 %add_convert_fusion.1 = (bf16[640,768]{1,0:T(8,128)(2,1)S(1)}, f32[640,768]{1,0:T(8,128)S(1)}) fusion(f32[640,768]{1,0:T(8,128)S(1)} %get-tuple-element.182, f32[]{:T(128)} %bitcast.5, f32[640,768]{1,0:T(8,128)S(1)} %copy-done.2, bf16[640,768]{1,0:T(8,128)(2,1)} %collective-permute-done.10, f32[640,768]{1,0:T(8,128)} %get-tuple-element.120, ...), kind=kLoop, calls=%fused_computation.15 | loop fusion | flops 3932160 | bytes 11796484 | tf_op jit(solution)/shard_map/convert
  327.5 3.6 multiply_reduce_fusion
  335.4 2.3 convert_add_fusion.1
  337.7 7.1 %collective-permute-done.21 = bf16[320,768]{1,0:T(8,128)(2,1)} collective-permute-done((bf16[320,768]{1,0:T(8,128)(2,1)S(1)}, bf16[320,768]{1,0:T(8,128)(2,1)}, u32[]{:S(2)}, u32[]{:S(2)}) %collective-permute-start.21) | collective-permute-done | bytes 491552 | tf_op jit(solution)/shard_map/ppermute | solution.py:475
  344.8 3.8 all-to-all-done
  348.6 2.4 multiply_reduce_fusion.5
  351.5 6.7 %multiply_reduce_fusion.2 = (f32[]{:T(128)}, f32[]{:T(128)}, f32[640,768]{1,0:T(8,128)}) fusion(f32[640,1536]{1,0:T(8,128)} %copy-done.4, f32[640,768]{1,0:T(8,128)} %get-tuple-element.180, f32[640,768]{1,0:T(8,128)S(1)} %get-tuple-element.182, f32[640]{0:T(1024)S(1)} %fusion.5, f32[640,768]{1,0:T(8,128)S(1)} %copy-done.8, ...), kind=kLoop, calls=%fused_computation.5 | loop fusion | flops 12779518 | bytes 19677192 | tf_op jit(solution)/shard_map/reduce_sum | solution.py:774
  358.2 2.7 stack.46
  363.7 1.6 slice.146
  369.1 5.1 %multiply_add_fusion.1 = (f32[640,768]{1,0:T(8,128)S(1)}, f32[640,768]{1,0:T(8,128)S(1)}) fusion(f32[640,768]{1,0:T(8,128)} %get-tuple-element.174, f32[640,1536]{1,0:T(8,128)} %copy-done.6, f32[]{:T(128)} %bitcast.23, f32[]{:T(128)} %bitcast, f32[]{:T(128)} %bitcast.24, f32[]{:T(128)} %bitcast.1), kind=kLoop, calls=%fused_computation.10 | loop fusion | flops 2949120 | bytes 7864336 | tf_op jit(solution)/shard_map/add | solution.py:766
  374.3 2.5 pad_maximum_fusion
  (224 shorter events, 69.2 us)
Async XLA Ops:
  7.2 6.0 %copy-start.44 = (f32[96,2,768]{2,1,0:T(2,128)S(1)}, f32[96,2,768]{2,1,0:T(2,128)}, u32[]{:S(2)}) copy-start(f32[96,2,768]{2,1,0:T(2,128)} %param.15) | copy-start | bytes 1769476
  7.2 6.2 %copy-start.26 = (bf16[640,1536]{1,0:T(8,128)(2,1)S(1)}, bf16[640,1536]{1,0:T(8,128)(2,1)}, u32[]{:S(2)}) copy-start(bf16[640,1536]{1,0:T(8,128)(2,1)} %param.11) | copy-start | bytes 5898244
  7.2 129.3 %all-gather.2.cloned.1.call-start = ((), (), s32[]{:S(2)}) async-start(), calls=%async_computation.2 | async-start | bytes 3981312 | tf_op jit(solution)/shard_map/all_gather | solution.py:696
  62.2 253.7 %reduce-scatter.2.cloned.1.call-start = ((), (), s32[]{:S(2)}) async-start(), calls=%async_computation.3 | async-start | bytes 3981312 | tf_op jit(solution)/shard_map/reduce_scatter | solution.py:721
  68.2 5.3 %copy-start.10 = (bf16[640,768]{1,0:T(8,128)(2,1)S(1)}, bf16[640,768]{1,0:T(8,128)(2,1)}, u32[]{:S(2)}) copy-start(bf16[640,768]{1,0:T(8,128)(2,1)} %multiply_convert_fusion.1.x) | copy-start | bytes 2949124
  68.2 79.0 %collective-permute-start.6 = (bf16[640,768]{1,0:T(8,128)(2,1)}, bf16[640,768]{1,0:T(8,128)(2,1)}, u32[]{:S(2)}, u32[]{:S(2)}) collective-permute-start(bf16[640,768]{1,0:T(8,128)(2,1)} %get-tuple-element.75.g_ref.refs_4_), channel_id=1, source_target_pairs={{0,1},{1,0},{2,3},{3,2},{4,5},{5,4},{6,7},{7,6},{8,9},{9,8},{10,11... | collective-permute-start | bytes 2949128 | tf_op jit(solution)/shard_map/ppermute | solution.py:475
  68.7 45.6 %collective-permute-start = (bf16[640,768]{1,0:T(8,128)(2,1)}, bf16[640,768]{1,0:T(8,128)(2,1)}, u32[]{:S(2)}, u32[]{:S(2)}) collective-permute-start(bf16[640,768]{1,0:T(8,128)(2,1)} %get-tuple-element.75.g_ref.refs_4_), channel_id=1, source_target_pairs={{0,2},{1,3},{2,0},{3,1},{4,6},{5,7},{6,4},{7,5},{8,10},{9,11},{10,... | collective-permute-start | bytes 2949128 | tf_op jit(solution)/shard_map/ppermute | solution.py:475
  114.3 18.2 %copy-start.16 = (bf16[1,8,96,192]{3,2,1,0:T(8,128)(2,1)}, bf16[1,8,96,192]{3,2,1,0:T(8,128)(2,1)S(1)}, u32[]{:S(2)}) copy-start(bf16[1,8,96,192]{3,2,1,0:T(8,128)(2,1)S(1)} %get-tuple-element.192) | copy-start | bytes 884740
  115.4 17.5 %collective-permute-start.3 = (bf16[640,192]{1,0:T(8,128)(2,1)S(1)}, bf16[640,192]{1,0:T(8,128)(2,1)S(1)}, u32[]{:S(2)}, u32[]{:S(2)}) collective-permute-start(bf16[640,192]{1,0:T(8,128)(2,1)S(1)} %get-tuple-element.195), channel_id=1, source_target_pairs={{0,3},{1,2},{2,1},{3,0},{4,7},{5,6},{6,5},{7,4},{8,11},{9,10},{10,... | collective-permute-start | bytes 737288 | tf_op jit(solution)/shard_map/ppermute | solution.py:475
  115.4 17.0 %collective-permute-start.2 = (bf16[640,192]{1,0:T(8,128)(2,1)S(1)}, bf16[640,192]{1,0:T(8,128)(2,1)S(1)}, u32[]{:S(2)}, u32[]{:S(2)}) collective-permute-start(bf16[640,192]{1,0:T(8,128)(2,1)S(1)} %get-tuple-element.196), channel_id=1, source_target_pairs={{0,2},{1,3},{2,0},{3,1},{4,6},{5,7},{6,4},{7,5},{8,10},{9,11},{10,... | collective-permute-start | bytes 737288 | tf_op jit(solution)/shard_map/ppermute | solution.py:475
  116.9 1.6 collective-permute-start.1
  118.5 13.9 %copy-start.30 = (bf16[640,192]{1,0:T(8,128)(2,1)}, bf16[640,192]{1,0:T(8,128)(2,1)S(1)}, u32[]{:S(2)}) copy-start(bf16[640,192]{1,0:T(8,128)(2,1)S(1)} %collective-permute-done.1) | copy-start | bytes 737284
  135.7 11.6 %collective-permute-start.5 = (bf16[640,768]{1,0:T(8,128)(2,1)S(1)}, bf16[640,768]{1,0:T(8,128)(2,1)}, u32[]{:S(2)}, u32[]{:S(2)}) collective-permute-start(bf16[640,768]{1,0:T(8,128)(2,1)S(1)} %multiply_convert_fusion.x_ref.refs_0_), channel_id=1, source_target_pairs={{0,1},{1,0},{2,3},{3,2},{4,5},{5,4},{6,7},{7,6},{8,9},{9,8},{10,11... | collective-permute-start | bytes 2949128 | tf_op jit(solution)/shard_map/ppermute | solution.py:475
  135.8 24.2 %collective-permute-start.4 = (bf16[640,768]{1,0:T(8,128)(2,1)S(1)}, bf16[640,768]{1,0:T(8,128)(2,1)}, u32[]{:S(2)}, u32[]{:S(2)}) collective-permute-start(bf16[640,768]{1,0:T(8,128)(2,1)S(1)} %multiply_convert_fusion.x_ref.refs_0_), channel_id=1, source_target_pairs={{0,2},{1,3},{2,0},{3,1},{4,6},{5,7},{6,4},{7,5},{8,10},{9,11},{10,... | collective-permute-start | bytes 2949128 | tf_op jit(solution)/shard_map/ppermute | solution.py:475
  136.4 23.7 %collective-permute-start.8 = (bf16[640,768]{1,0:T(8,128)(2,1)}, bf16[640,768]{1,0:T(8,128)(2,1)}, u32[]{:S(2)}, u32[]{:S(2)}) collective-permute-start(bf16[640,768]{1,0:T(8,128)(2,1)} %collective-permute-done.g_ref.refs_6_), channel_id=1, source_target_pairs={{0,1},{1,0},{2,3},{3,2},{4,5},{5,4},{6,7},{7,6},{8,9},{9,8},{10,11... | collective-permute-start | bytes 2949128 | tf_op jit(solution)/shard_map/ppermute | solution.py:475
  160.0 2.8 collective-permute-start.7
  174.8 10.8 %collective-permute-start.12 = (bf16[640,768]{1,0:T(8,128)(2,1)}, bf16[640,768]{1,0:T(8,128)(2,1)S(1)}, u32[]{:S(2)}, u32[]{:S(2)}) collective-permute-start(bf16[640,768]{1,0:T(8,128)(2,1)} %get-tuple-element.87), channel_id=1, source_target_pairs={{0,1},{1,0},{2,3},{3,2},{4,5},{5,4},{6,7},{7,6},{8,9},{9,8},{10,11... | collective-permute-start | bytes 2949128 | tf_op jit(solution)/shard_map/ppermute | solution.py:475
  188.0 26.0 %collective-permute-start.13 = (bf16[640,768]{1,0:T(8,128)(2,1)}, bf16[640,768]{1,0:T(8,128)(2,1)}, u32[]{:S(2)}, u32[]{:S(2)}) collective-permute-start(bf16[640,768]{1,0:T(8,128)(2,1)} %add_convert_fusion.3), channel_id=1, source_target_pairs={{0,2},{1,3},{2,0},{3,1},{4,6},{5,7},{6,4},{7,5},{8,10},{9,11},{10,... | collective-permute-start | bytes 2949128 | tf_op jit(solution)/shard_map/ppermute | solution.py:475
  188.5 25.5 %collective-permute-start.11 = (bf16[640,768]{1,0:T(8,128)(2,1)}, bf16[640,768]{1,0:T(8,128)(2,1)}, u32[]{:S(2)}, u32[]{:S(2)}) collective-permute-start(bf16[640,768]{1,0:T(8,128)(2,1)} %get-tuple-element.85), channel_id=1, source_target_pairs={{0,1},{1,0},{2,3},{3,2},{4,5},{5,4},{6,7},{7,6},{8,9},{9,8},{10,11... | collective-permute-start | bytes 2949128 | tf_op jit(solution)/shard_map/ppermute | solution.py:475
  188.6 47.9 %collective-permute-start.9 = (f32[640,768]{1,0:T(8,128)}, f32[640,768]{1,0:T(8,128)}, u32[]{:S(2)}, u32[]{:S(2)}) collective-permute-start(f32[640,768]{1,0:T(8,128)} %get-tuple-element.83), channel_id=1, source_target_pairs={{0,1},{1,0},{2,3},{3,2},{4,5},{5,4},{6,7},{7,6},{8,9},{9,8},{10,11... | collective-permute-start | bytes 5898248 | tf_op jit(solution)/shard_map/ppermute | solution.py:475
  234.6 10.0 %collective-permute-start.16 = (bf16[640,192]{1,0:T(8,128)(2,1)S(1)}, bf16[640,192]{1,0:T(8,128)(2,1)S(1)}, u32[]{:S(2)}, u32[]{:S(2)}) collective-permute-start(bf16[640,192]{1,0:T(8,128)(2,1)S(1)} %copy.66), channel_id=1, source_target_pairs={{0,3},{1,2},{2,1},{3,0},{4,7},{5,6},{6,5},{7,4},{8,11},{9,10},{10,... | collective-permute-start | bytes 737288 | tf_op jit(solution)/shard_map/ppermute | solution.py:475
  235.7 16.1 %collective-permute-start.15 = (bf16[640,192]{1,0:T(8,128)(2,1)}, bf16[640,192]{1,0:T(8,128)(2,1)S(1)}, u32[]{:S(2)}, u32[]{:S(2)}) collective-permute-start(bf16[640,192]{1,0:T(8,128)(2,1)} %copy.65), channel_id=1, source_target_pairs={{0,2},{1,3},{2,0},{3,1},{4,6},{5,7},{6,4},{7,5},{8,10},{9,11},{10,... | collective-permute-start | bytes 737288 | tf_op jit(solution)/shard_map/ppermute | solution.py:475
  236.3 21.0 %collective-permute-start.14 = (bf16[640,192]{1,0:T(8,128)(2,1)}, bf16[640,192]{1,0:T(8,128)(2,1)S(1)}, u32[]{:S(2)}, u32[]{:S(2)}) collective-permute-start(bf16[640,192]{1,0:T(8,128)(2,1)} %copy.64), channel_id=1, source_target_pairs={{0,1},{1,0},{2,3},{3,2},{4,5},{5,4},{6,7},{7,6},{8,9},{9,8},{10,11... | collective-permute-start | bytes 737288 | tf_op jit(solution)/shard_map/ppermute | solution.py:475
  236.6 15.3 %copy-start.28 = (bf16[640,192]{1,0:T(8,128)(2,1)S(1)}, bf16[640,192]{1,0:T(8,128)(2,1)}, u32[]{:S(2)}) copy-start(bf16[640,192]{1,0:T(8,128)(2,1)} %copy-done.27) | copy-start | bytes 737284
  236.6 17.2 %copy-start.33 = (bf16[640,192]{1,0:T(8,128)(2,1)S(1)}, bf16[640,192]{1,0:T(8,128)(2,1)}, u32[]{:S(2)}) copy-start(bf16[640,192]{1,0:T(8,128)(2,1)} %copy-done.32) | copy-start | bytes 737284
  240.0 15.7 %copy-start.31 = (bf16[640,192]{1,0:T(8,128)(2,1)S(1)}, bf16[640,192]{1,0:T(8,128)(2,1)}, u32[]{:S(2)}) copy-start(bf16[640,192]{1,0:T(8,128)(2,1)} %copy-done.30) | copy-start | bytes 737284
  240.0 54.5 %collective-permute-start.10 = (bf16[640,768]{1,0:T(8,128)(2,1)}, bf16[640,768]{1,0:T(8,128)(2,1)}, u32[]{:S(2)}, u32[]{:S(2)}) collective-permute-start(bf16[640,768]{1,0:T(8,128)(2,1)} %add_convert_fusion.4), channel_id=1, source_target_pairs={{0,2},{1,3},{2,0},{3,1},{4,6},{5,7},{6,4},{7,5},{8,10},{9,11},{10,... | collective-permute-start | bytes 2949128 | tf_op jit(solution)/shard_map/ppermute | solution.py:475
  244.6 12.3 %copy-start.50 = (bf16[640,192]{1,0:T(8,128)(2,1)}, bf16[640,192]{1,0:T(8,128)(2,1)S(1)}, u32[]{:S(2)}) copy-start(bf16[640,192]{1,0:T(8,128)(2,1)S(1)} %collective-permute-done.16.refs_7_) | copy-start | bytes 737284
  251.9 5.0 %copy-start.51 = (bf16[640,192]{1,0:T(8,128)(2,1)}, bf16[640,192]{1,0:T(8,128)(2,1)S(1)}, u32[]{:S(2)}) copy-start(bf16[640,192]{1,0:T(8,128)(2,1)S(1)} %collective-permute-done.15.refs_6_) | copy-start | bytes 737284
  253.0 39.0 %collective-permute-start.19 = (bf16[768,192]{0,1:T(8,128)(2,1)}, bf16[768,192]{0,1:T(8,128)(2,1)}, u32[]{:S(2)}, u32[]{:S(2)}) collective-permute-start(bf16[768,192]{0,1:T(8,128)(2,1)} %convolution_convert_fusion.8), channel_id=1, source_target_pairs={{0,3},{1,2},{2,1},{3,0},{4,7},{5,6},{6,5},{7,4},{8,11},{9,10},{10,... | collective-permute-start | bytes 884744 | tf_op jit(solution)/shard_map/ppermute | solution.py:475
  255.0 37.0 %collective-permute-start.18 = (bf16[768,192]{0,1:T(8,128)(2,1)}, bf16[768,192]{0,1:T(8,128)(2,1)}, u32[]{:S(2)}, u32[]{:S(2)}) collective-permute-start(bf16[768,192]{0,1:T(8,128)(2,1)} %convolution_convert_fusion.9), channel_id=1, source_target_pairs={{0,2},{1,3},{2,0},{3,1},{4,6},{5,7},{6,4},{7,5},{8,10},{9,11},{10,... | collective-permute-start | bytes 884744 | tf_op jit(solution)/shard_map/ppermute | solution.py:475
  256.9 35.1 %collective-permute-start.17 = (bf16[768,192]{0,1:T(8,128)(2,1)}, bf16[768,192]{0,1:T(8,128)(2,1)}, u32[]{:S(2)}, u32[]{:S(2)}) collective-permute-start(bf16[768,192]{0,1:T(8,128)(2,1)} %convolution_convert_fusion.10), channel_id=1, source_target_pairs={{0,1},{1,0},{2,3},{3,2},{4,5},{5,4},{6,7},{7,6},{8,9},{9,8},{10,11... | collective-permute-start | bytes 884744 | tf_op jit(solution)/shard_map/ppermute | solution.py:475
  258.0 34.0 %copy-start.29 = (bf16[640,192]{1,0:T(8,128)(2,1)S(1)}, bf16[640,192]{1,0:T(8,128)(2,1)}, u32[]{:S(2)}) copy-start(bf16[640,192]{1,0:T(8,128)(2,1)} %get-tuple-element.103) | copy-start | bytes 737284
  296.7 2.6 collective-permute-start.20
  296.9 25.9 %collective-permute-start.24 = (f32[640,768]{1,0:T(8,128)}, f32[640,768]{1,0:T(8,128)}, u32[]{:S(2)}, u32[]{:S(2)}) collective-permute-start(f32[640,768]{1,0:T(8,128)} %get-tuple-element.121), channel_id=1, source_target_pairs={{0,1},{1,0},{2,3},{3,2},{4,5},{5,4},{6,7},{7,6},{8,9},{9,8},{10,11... | collective-permute-start | bytes 5898248 | tf_op jit(solution)/shard_map/ppermute | solution.py:475
  302.4 13.5 %collective-permute-start.22 = (bf16[320,768]{1,0:T(8,128)(2,1)}, bf16[320,768]{1,0:T(8,128)(2,1)S(1)}, u32[]{:S(2)}, u32[]{:S(2)}) collective-permute-start(bf16[320,768]{1,0:T(8,128)(2,1)} %get-tuple-element.198), channel_id=1, source_target_pairs={{0,2},{1,3},{2,0},{3,1},{4,6},{5,7},{6,4},{7,5},{8,10},{9,11},{10,... | collective-permute-start | bytes 1474568 | tf_op jit(solution)/shard_map/ppermute | solution.py:475
  314.6 5.7 %copy-start.21 = (bf16[640,576]{1,0:T(8,128)(2,1)S(1)}, bf16[640,576]{1,0:T(8,128)(2,1)}, u32[]{:S(2)}) copy-start(bf16[640,576]{1,0:T(8,128)(2,1)} %get-tuple-element.112) | copy-start | bytes 2211844
  315.8 32.8 %all-to-all-start = ((bf16[8,96,768]{2,1,0:T(8,128)(2,1)}), bf16[8,96,768]{2,1,0:T(8,128)(2,1)}, u32[]{:S(2)}, u32[]{:S(2)}) async-start(bf16[8,96,768]{2,1,0:T(8,128)(2,1)} %pad_maximum_fusion.2), calls=%async_computation.1 | async-start | bytes 2359296 | tf_op jit(solution)/shard_map/all_to_all | solution.py:749
  322.6 12.7 %collective-permute-start.23 = (bf16[640,768]{1,0:T(8,128)(2,1)S(1)}, bf16[640,768]{1,0:T(8,128)(2,1)S(1)}, u32[]{:S(2)}, u32[]{:S(2)}) collective-permute-start(bf16[640,768]{1,0:T(8,128)(2,1)S(1)} %convolution_convert_fusion), channel_id=1, source_target_pairs={{0,1},{1,0},{2,3},{3,2},{4,5},{5,4},{6,7},{7,6},{8,9},{9,8},{10,11... | collective-permute-start | bytes 2949128 | tf_op jit(solution)/shard_map/ppermute | solution.py:475
  322.7 4.5 %copy-start.5 = (f32[640,1536]{1,0:T(8,128)S(1)}, f32[640,1536]{1,0:T(8,128)}, u32[]{:S(2)}) copy-start(f32[640,1536]{1,0:T(8,128)} %copy-done.4) | copy-start | bytes 11796484
  322.8 4.8 %copy-start.7 = (f32[640,1536]{1,0:T(8,128)S(1)}, f32[640,1536]{1,0:T(8,128)}, u32[]{:S(2)}) copy-start(f32[640,1536]{1,0:T(8,128)} %copy-done.6) | copy-start | bytes 11796484
  331.1 13.7 %collective-permute-start.21 = (bf16[320,768]{1,0:T(8,128)(2,1)S(1)}, bf16[320,768]{1,0:T(8,128)(2,1)}, u32[]{:S(2)}, u32[]{:S(2)}) collective-permute-start(bf16[320,768]{1,0:T(8,128)(2,1)S(1)} %copy-done.45), channel_id=1, source_target_pairs={{0,2},{1,3},{2,0},{3,1},{4,6},{5,7},{6,4},{7,5},{8,10},{9,11},{10,... | collective-permute-start | bytes 1474568 | tf_op jit(solution)/shard_map/ppermute | solution.py:475
  337.7 13.4 %copy-start.14 = (bf16[640,768]{1,0:T(8,128)(2,1)S(1)}, bf16[640,768]{1,0:T(8,128)(2,1)}, u32[]{:S(2)}) copy-start(bf16[640,768]{1,0:T(8,128)(2,1)} %get-tuple-element.84) | copy-start | bytes 2949124
  360.9 1.2 collective-permute-start.25
  362.1 5.4 %collective-permute-start.26 = (f32[3,768]{1,0:T(4,128)S(1)}, f32[3,768]{1,0:T(4,128)S(1)}, u32[]{:S(2)}, u32[]{:S(2)}) collective-permute-start(f32[3,768]{1,0:T(4,128)S(1)} %fusion.6), channel_id=1, source_target_pairs={{0,2},{1,3},{2,0},{3,1},{4,6},{5,7},{6,4},{7,5},{8,10},{9,11},{10,... | collective-permute-start | bytes 27656 | tf_op jit(solution)/shard_map/ppermute | solution.py:670
  367.6 6.6 %collective-permute-start.27 = (f32[3,768]{1,0:T(4,128)S(1)}, f32[3,768]{1,0:T(4,128)S(1)}, u32[]{:S(2)}, u32[]{:S(2)}) collective-permute-start(f32[3,768]{1,0:T(4,128)S(1)} %fusion.64), channel_id=1, source_target_pairs={{0,4},{4,0},{8,12},{12,8},{16,20},{20,16},{24,28},{28,24},{1,5},{5... | collective-permute-start | bytes 27656 | tf_op jit(solution)/shard_map/ppermute | solution.py:670
  374.2 3.8 collective-permute-start.28
  378.0 4.6 %collective-permute-start.29 = (f32[3,768]{1,0:T(4,128)S(1)}, f32[3,768]{1,0:T(4,128)S(1)}, u32[]{:S(2)}, u32[]{:S(2)}) collective-permute-start(f32[3,768]{1,0:T(4,128)S(1)} %add.168), channel_id=1, source_target_pairs={{0,16},{4,20},{8,24},{12,28},{16,0},{20,4},{24,8},{28,12},{1,17},{... | collective-permute-start | bytes 27656 | tf_op jit(solution)/shard_map/ppermute | solution.py:670
  (38 other events, 88.2 us)
Sparse Core Ops, SparseCore 0:
  62.3 62.8 all-gather.1
  214.1 76.6 reduce-scatter.1
